TPU v7x, 32 devices: a whole 2x2x4 slice. The times are simulated.
32 devices in a mesh: grp: 2 (over x), ref: 16 (over z, y, core).
Axes of the slice: x: 2, y: 2, z: 4, core: 2. Of those that a mesh axis runs over, the one named last changes fastest.
Arguments:
- particles: bfloat16 [256, 512], P(('grp', 'ref')), may hold values from -30 to 30
- samples: bfloat16 [65536, 512], P('ref'), may hold values from -6 to 6
Outputs:
- moved: float32 [256, 512], P(('grp', 'ref'))
All inputs are finite; a program needn't handle non-finite values.
Results may differ from a plain program's by a relative error of at most 0.0035.
Values may be sent and summed in bfloat16 or wider, within the bound.
No kernel may reach another device: no remote copies, remote signals or barrier semaphores. Data moves between devices by JAX's collectives and lax.ppermute only.
A program may use at most 128 MiB of HBM per device.

v0:
```python
import functools

import jax
import jax.numpy as jnp
from jax import lax
from jax.experimental import pallas as pl
from jax.experimental.pallas import tpu as pltpu
from jax.sharding import PartitionSpec as P


KERNEL_WIDTH = 16
STEP_SIZE = 8.0
LANES = 128
NT = (((1,), (1,)), ((), ()))
VMEM = pl.BlockSpec(memory_space=pltpu.VMEM)
ANY = pl.BlockSpec(memory_space=pl.ANY)
HBM = pl.BlockSpec(memory_space=pltpu.HBM)
SMALL = 2 << 20
F32 = jnp.float32
BF16 = jnp.bfloat16
HALF = 1.0 / (2.0 * KERNEL_WIDTH)


def lane_square_norms(values):
    partial = None
    for start in range(0, values.shape[1], LANES):
        wide = values[:, start : start + LANES].astype(F32)
        partial = wide * wide if partial is None else partial + wide * wide
    high = partial.astype(BF16)
    rest = partial - high.astype(F32)
    mid = rest.astype(BF16)
    low = (rest - mid.astype(F32)).astype(BF16)
    ones = jnp.ones((8, LANES), BF16)

    def summed(part):
        return lax.dot_general(ones, part, NT, preferred_element_type=F32)

    return summed(low) + summed(mid) + summed(high)


def turned_block(block, turned_ref, norm_ref, columns):
    turned = jnp.transpose(block)
    turned_ref[:, columns] = turned
    wide = turned.astype(F32)
    norm = jnp.sum(wide * wide, axis=0, keepdims=True) * HALF
    norm_ref[:, columns] = jnp.broadcast_to(norm, (8, norm.shape[1]))


def prepare_kernel(first, samples_ref, *refs):
    turned_ref, norm_ref = refs[-2:]
    count = turned_ref.shape[1]
    tile = min(512, count)
    for start in range(0, count, tile):
        block = samples_ref[pl.ds(first + start, tile), :]
        turned_block(block, turned_ref, norm_ref, pl.ds(start, tile))


def prepare(samples, first, count, after=()):
    width = samples.shape[1]
    return pl.pallas_call(
        functools.partial(prepare_kernel, first),
        out_shape=(
            jax.ShapeDtypeStruct((width, count), samples.dtype),
            jax.ShapeDtypeStruct((8, count), F32),
        ),
        in_specs=[VMEM] + [ANY] * len(after),
        out_specs=(VMEM, VMEM),
        compiler_params=pltpu.CompilerParams(vmem_limit_bytes=SMALL),
        cost_estimate=pl.CostEstimate(
            flops=2 * count * width, bytes_accessed=4 * count * width, transcendentals=0
        ),
        name="prepare",
    )(samples, *after)


def stage_kernel(own_ref, samples_ref, own_out, samples_out, turned_out, norm_out, sems):
    count = samples_ref.shape[0]
    chunks = sems.shape[0] - 1
    size = count // chunks
    own_copy = pltpu.make_async_copy(own_ref, own_out, sems.at[chunks])
    own_copy.start()
    copies = []
    for k in range(chunks):
        rows = pl.ds(k * size, size)
        copies.append(
            pltpu.make_async_copy(samples_ref.at[rows], samples_out.at[rows], sems.at[k])
        )
        copies[-1].start()
    own_copy.wait()
    for k in range(chunks):
        copies[k].wait()
        if k * size < norm_out.shape[1]:
            rows = pl.ds(k * size, size)
            turned_block(samples_out[rows, :], turned_out, norm_out, rows)


def in_hbm(array):
    return pltpu.with_memory_space_constraint(array, pltpu.HBM)


def stage(own, samples, first_count, chunks):
    return pl.pallas_call(
        stage_kernel,
        out_shape=(
            pltpu.VMEM(own.shape, own.dtype),
            pltpu.VMEM(samples.shape, samples.dtype),
            pltpu.VMEM((samples.shape[1], first_count), samples.dtype),
            pltpu.VMEM((8, first_count), F32),
        ),
        in_specs=[HBM, HBM],
        out_specs=(VMEM, VMEM, VMEM, VMEM),
        scratch_shapes=[pltpu.SemaphoreType.DMA((chunks + 1,))],
        compiler_params=pltpu.CompilerParams(vmem_limit_bytes=SMALL),
        name="stage",
    )(in_hbm(own), in_hbm(samples))


def join_kernel(first_ref, second_ref, *refs):
    refs[-1][...] = jnp.concatenate([first_ref[...], second_ref[...]], axis=0)


def join(first, second, after=()):
    rows, width = first.shape
    return pl.pallas_call(
        join_kernel,
        out_shape=jax.ShapeDtypeStruct((2 * rows, width), first.dtype),
        in_specs=[VMEM, VMEM] + [ANY] * len(after),
        out_specs=VMEM,
        compiler_params=pltpu.CompilerParams(vmem_limit_bytes=SMALL),
        name="join",
    )(first, second, *after)


def packed(ref, sums, top, total):
    width = sums.shape[1]
    lane_id = lax.broadcasted_iota(jnp.int32, (sums.shape[0], LANES), 1)
    ref[:, 0:width] = sums
    ref[:, width : width + LANES] = jnp.where(lane_id < LANES // 2, top, total)


def cross_kernel(near_ref, far_ref, samples_ref, *refs):
    near_out, far_out = refs[-2:]
    turned_refs, norm_refs = refs[0:-2:2], refs[1:-2:2]
    group = jnp.concatenate([near_ref[...], far_ref[...]], axis=0)
    rows, _ = group.shape
    wide = group.astype(F32)
    group_sq = jnp.sum(wide * wide, axis=1, keepdims=True) * HALF
    scaled = group * BF16(2.0 * HALF)
    tiles, start = [], 0
    for first, last in ((0, 1), (1, len(turned_refs))):
        chunks = []
        for turned_ref, norm_ref in zip(turned_refs[first:last], norm_refs[first:last]):
            dots = jnp.dot(scaled, turned_ref[...], preferred_element_type=F32)
            chunks.append(dots - norm_ref[0:1, :])
        scores = jnp.concatenate(chunks, axis=1)
        count = scores.shape[1]
        lanes = [slice(lane, lane + LANES) for lane in range(0, count, LANES)]
        peak = functools.reduce(jnp.maximum, [scores[:, lane] for lane in lanes])
        top = jnp.max(peak, axis=1, keepdims=True)
        weights = jnp.exp(scores - top)
        partial = functools.reduce(jnp.add, [weights[:, lane] for lane in lanes])
        sums = jnp.dot(
            weights.astype(BF16), samples_ref[pl.ds(start, count), :], preferred_element_type=F32
        )
        tiles.append((top, partial, sums))
        start += count
    top = jnp.maximum(tiles[0][0], tiles[1][0])
    scales = [jnp.exp(tile[0] - top) for tile in tiles]
    partial = sum(tile[1] * scale for tile, scale in zip(tiles, scales))
    sums = sum(tile[2] * scale for tile, scale in zip(tiles, scales))
    total = jnp.sum(partial, axis=1, keepdims=True)
    top = top - group_sq
    half = rows // 2
    packed(near_out, sums[:half], top[:half], total[:half])
    packed(far_out, sums[half:], top[half:], total[half:])


def cross_terms(near, far, samples, prepared):
    count, width = samples.shape
    rows = near.shape[0] + far.shape[0]
    part = jax.ShapeDtypeStruct((rows // 2, width + LANES), F32)
    return pl.pallas_call(
        cross_kernel,
        out_shape=(part, part),
        in_specs=[VMEM] * (3 + 2 * len(prepared)),
        out_specs=(VMEM, VMEM),
        compiler_params=pltpu.CompilerParams(vmem_limit_bytes=12 << 20),
        cost_estimate=pl.CostEstimate(
            flops=4 * rows * count * width,
            bytes_accessed=4 * count * width,
            transcendentals=rows * count,
        ),
        name="cross_terms",
    )(near, far, samples, *[array for pair in prepared for array in pair])


def split_stats(stats):
    lane_id = lax.broadcasted_iota(jnp.int32, stats.shape, 1)
    left = lane_id < LANES // 2
    turned = pltpu.roll(stats, LANES // 2, 1)
    return jnp.where(left, stats, turned), jnp.where(left, turned, stats)


def three_parts(values):
    high = values.astype(BF16).astype(F32)
    rest = values - high
    mid = rest.astype(BF16).astype(F32)
    return high, mid, rest - mid


def parcel(ref, sums, top, total):
    lane_id = lax.broadcasted_iota(jnp.int32, top.shape, 1)
    stats = jnp.zeros_like(top)
    for index, part in enumerate(three_parts(top) + three_parts(total)):
        stats = jnp.where(lane_id == index, part, stats)
    for index, tile in enumerate(sums + [stats]):
        ref[:, pl.ds(index * LANES, LANES)] = tile.astype(BF16)


def opened(ref):
    tiles = [
        ref[:, pl.ds(lane, LANES)].astype(F32) for lane in range(0, ref.shape[1], LANES)
    ]
    stats = tiles.pop()
    parts = [jnp.broadcast_to(stats[:, k : k + 1], stats.shape) for k in range(6)]
    return tiles, parts[2] + parts[1] + parts[0], parts[5] + parts[4] + parts[3]


def loaded(ref):
    width = ref.shape[1] - LANES
    top, total = split_stats(ref[:, width : width + LANES])
    return [ref[:, pl.ds(lane, LANES)] for lane in range(0, width, LANES)], top, total


def combined(parts):
    tops = [part[1] for part in parts]
    top = functools.reduce(jnp.maximum, tops)
    scales = [jnp.exp(one - top) for one in tops]
    sums = [
        sum(tile * scale for tile, scale in zip(tiles, scales))
        for tiles in zip(*[part[0] for part in parts])
    ]
    return sums, top, sum(part[2] * scale for part, scale in zip(parts, scales))


def halves(sums, top, total, keep_ref, send_ref):
    half = keep_ref.shape[0]
    packed(
        keep_ref,
        jnp.concatenate([tile[:half] for tile in sums], axis=1),
        top[:half],
        total[:half],
    )
    parcel(send_ref, [tile[half:] for tile in sums], top[half:], total[half:])


def first_combine_kernel(left_ref, right_ref, centre_ref, keep_ref, send_ref):
    sums, top, total = combined([loaded(left_ref), loaded(right_ref)])
    sums = [
        tile - total * centre_ref[:, pl.ds(index * LANES, LANES)]
        for index, tile in enumerate(sums)
    ]
    halves(sums, top, total, keep_ref, send_ref)


def next_combine_kernel(left_ref, right_ref, keep_ref, send_ref):
    halves(*combined([loaded(left_ref), opened(right_ref)]), keep_ref, send_ref)


def combine(left, right, centres=None):
    rows, width = left.shape[0] // 2, left.shape[1]
    more = () if centres is None else (centres,)
    return pl.pallas_call(
        next_combine_kernel if centres is None else first_combine_kernel,
        out_shape=(
            jax.ShapeDtypeStruct((rows, width), F32),
            jax.ShapeDtypeStruct((rows, width), BF16),
        ),
        in_specs=[VMEM] * (2 + len(more)),
        out_specs=(VMEM, VMEM),
        compiler_params=pltpu.CompilerParams(vmem_limit_bytes=SMALL),
        name="combine",
    )(left, right, *more)


def self_kernel(near_ref, far_ref, *refs):
    visits = (len(refs) - 2) // 2
    visit_refs, centre_ref, out_refs = refs[:visits], refs[visits], refs[visits + 1 :]
    near = near_ref.shape[0]
    rows = jnp.concatenate([near_ref[...]] + [ref[...] for ref in visit_refs], axis=0)
    wide = rows.astype(F32)
    rows_sq = jnp.sum(wide * wide, axis=1, keepdims=True) * HALF
    scaled = rows * BF16(2.0 * HALF)
    columns = jnp.concatenate([near_ref[...], far_ref[...]], axis=0)
    dots = lax.dot_general(scaled, columns, NT, preferred_element_type=F32)
    scores = dots - rows_sq - lane_square_norms(columns)[0:1] * HALF
    row_id = lax.broadcasted_iota(jnp.int32, scores.shape, 0)
    same = (row_id == lax.broadcasted_iota(jnp.int32, scores.shape, 1)) & (row_id < near)
    scores = jnp.where(same, -1e30, scores)
    top = jnp.max(scores, axis=1, keepdims=True)
    weights = jnp.where(same, 0.0, jnp.exp(scores - top))
    total = jnp.sum(weights, axis=1, keepdims=True)
    sums = jnp.dot(weights.astype(BF16), columns, preferred_element_type=F32)
    centre_ref[...] = sums[:near] / total[:near]
    size = out_refs[0].shape[0]
    for first, ref in zip([0] + [near + k * size for k in range(visits)], out_refs):
        here = slice(first, first + size)
        packed(ref, sums[here], top[here], total[here])


def self_terms(near, far, visitors, size):
    width = near.shape[1]
    part = jax.ShapeDtypeStruct((size, width + LANES), F32)
    return pl.pallas_call(
        self_kernel,
        out_shape=(jax.ShapeDtypeStruct(near.shape, F32),) + (part,) * (1 + len(visitors)),
        in_specs=[VMEM] * (2 + len(visitors)),
        out_specs=(VMEM,) * (2 + len(visitors)),
        compiler_params=pltpu.CompilerParams(vmem_limit_bytes=SMALL),
        name="self_terms",
    )(near, far, *visitors)


def final_kernel(own_ref, left_ref, right_ref, centre_ref, *refs):
    self_refs, out_ref = refs[:-1], refs[-1]
    rows = own_ref.shape[0]
    sums, _, total = combined([loaded(left_ref), opened(right_ref)])
    self_sums, _, self_total = combined([loaded(ref) for ref in self_refs])
    scale = 1.0 / total
    self_scale = 1.0 / self_total
    for index, (tile, self_tile) in enumerate(zip(sums, self_sums)):
        lanes = pl.ds(index * LANES, LANES)
        cross_mean = tile * scale + centre_ref[0:rows, lanes]
        out_ref[:, lanes] = own_ref[:, lanes].astype(F32) + STEP_SIZE * (
            cross_mean - self_tile * self_scale
        )


def final(own, left, right, centres, self_parts):
    return pl.pallas_call(
        final_kernel,
        out_shape=jax.ShapeDtypeStruct(own.shape, F32),
        in_specs=[VMEM] * (4 + len(self_parts)),
        out_specs=VMEM,
        compiler_params=pltpu.CompilerParams(vmem_limit_bytes=SMALL),
        name="final",
    )(own, left, right, centres, *self_parts)


def swap(values, mask):
    size = lax.axis_size("ref")
    return lax.ppermute(values, "ref", [(i, i ^ mask) for i in range(size)])


def across(values, shift):
    groups, size = lax.axis_size("grp"), lax.axis_size("ref")
    pairs = [
        (g * size + i, (g + shift) % groups * size + (i ^ 1))
        for g in range(groups)
        for i in range(size)
    ]
    return lax.ppermute(values, ("grp", "ref"), pairs)


def swap_masks(size):
    count = size.bit_length() - 1
    assert size == 1 << count and count >= 3
    return [1] + [(1 << k) | 1 for k in range(1, count)]


def per_device(particles, samples):
    ref_size = lax.axis_size("ref")
    grp_size = lax.axis_size("grp")
    masks = swap_masks(ref_size)
    count = samples.shape[0]
    half = count // 2
    own, staged, *first_part = stage(particles, samples, half, 8)
    prepared = [first_part]
    block = own
    for mask in reversed(masks[1:]):
        other = swap(particles if block is own else block, mask)
        if block is not own and len(prepared) < 3:
            quarter = half // 2
            prepared.append(
                prepare(staged, half + (len(prepared) - 1) * quarter, quarter, [block])
            )
        block = join(block, other, prepared[-1][1:])
    far_block = swap(block, masks[0])
    keep, send = cross_terms(block, far_block, staged, prepared)
    visitors = [across(own, k) for k in range(1, grp_size)]
    centres, *self_parts = self_terms(block, far_block, visitors, own.shape[0])
    returned = [across(part, -k) for k, part in zip(range(1, grp_size), self_parts[1:])]
    keep, send = combine(keep, swap(send, masks[0]), centres)
    for mask in masks[1:-1]:
        keep, send = combine(keep, swap(send, mask))
    last = swap(send, masks[-1])
    return final(own, keep, last, centres, [self_parts[0]] + returned)


def solution(mesh):
    in_specs = (P(("grp", "ref"), None), P("ref", None))
    out_specs = P(("grp", "ref"), None)

    return jax.shard_map(
        per_device, mesh=mesh, in_specs=in_specs, out_specs=out_specs, check_vma=False
    )
```

profile of v0, /device:TPU:0, one launch (start us, length us, event | category | flops | bytes accessed | tf_op | source)
XLA Modules:
  0.0 31.8 jit_solution(15168963300007935835)
XLA Ops:
  0.0 3.5 %collective-permute-start = (bf16[8,512]{1,0:T(8,128)(2,1)}, bf16[8,512]{1,0:T(8,128)(2,1)S(1)}, u32[]{:S(2)}, u32[]{:S(2)}) collective-permute-start(bf16[8,512]{1,0:T(8,128)(2,1)} %own_ref.1), channel_id=1, source_target_pairs={{0,9},{1,8},{2,11},{3,10},{4,13},{5,12},{6,15},{7,14},{8,1},{9,0},... | collective-permute-start | bytes 24584 | tf_op jit(solution)/shard_map/ppermute | solution.py:352
  3.5 2.2 %stage.1 = (bf16[8,512]{1,0:T(8,128)(2,1)S(1)}, bf16[4096,512]{1,0:T(8,128)(2,1)S(1)}, bf16[512,2048]{1,0:T(8,128)(2,1)S(1)}, f32[8,2048]{1,0:T(8,128)S(1)}) custom-call(bf16[8,512]{1,0:T(8,128)(2,1)} %own_ref.1, bf16[4096,512]{1,0:T(8,128)(2,1)} %samples_ref.1), custom_call_target="tpu_custom_call" | custom-call | tf_op jit(solution)/shard_map/stage/pallas_call | solution.py:102
  5.8 0.0 collective-permute-done.second_ref
  5.8 1.9 %collective-permute-start.1 = (bf16[16,512]{1,0:T(8,128)(2,1)S(1)}, bf16[16,512]{1,0:T(8,128)(2,1)S(1)}, u32[]{:S(2)}, u32[]{:S(2)}) collective-permute-start(bf16[16,512]{1,0:T(8,128)(2,1)S(1)} %join.3.refs_0_.first_ref), channel_id=1, source_target_pairs={{0,5},{1,4},{2,7},{3,6},{4,1},{5,0},{6,3},{7,2},{8,13},{9,12},{10,... | collective-permute-start | bytes 49160 | tf_op jit(solution)/shard_map/ppermute | solution.py:352
  7.7 0.3 %prepare.2 = (bf16[512,1024]{1,0:T(8,128)(2,1)S(1)}, f32[8,1024]{1,0:T(8,128)S(1)}) custom-call(bf16[4096,512]{1,0:T(8,128)(2,1)S(1)} %get-tuple-element.26.samples_ref, bf16[16,512]{1,0:T(8,128)(2,1)S(1)} %join.3.refs_0_.first_ref), custom_call_target="tpu_custom_call" | custom-call | flops 1048576 | bytes 2097152 | tf_op jit(solution)/shard_map/prepare/pallas_call | solution.py:60
  8.0 1.1 %collective-permute-done.1.second_ref = bf16[16,512]{1,0:T(8,128)(2,1)S(1)} collective-permute-done((bf16[16,512]{1,0:T(8,128)(2,1)S(1)}, bf16[16,512]{1,0:T(8,128)(2,1)S(1)}, u32[]{:S(2)}, u32[]{:S(2)}) %collective-permute-start.1) | collective-permute-done | bytes 16416 | tf_op jit(solution)/shard_map/ppermute | solution.py:352
  9.1 1.7 %collective-permute-start.2 = (bf16[32,512]{1,0:T(8,128)(2,1)S(1)}, bf16[32,512]{1,0:T(8,128)(2,1)S(1)}, u32[]{:S(2)}, u32[]{:S(2)}) collective-permute-start(bf16[32,512]{1,0:T(8,128)(2,1)S(1)} %join.4.refs_0_.first_ref), channel_id=1, source_target_pairs={{0,3},{1,2},{2,1},{3,0},{4,7},{5,6},{6,5},{7,4},{8,11},{9,10},{10,... | collective-permute-start | bytes 98312 | tf_op jit(solution)/shard_map/ppermute | solution.py:352
  10.8 0.3 %prepare.3 = (bf16[512,1024]{1,0:T(8,128)(2,1)S(1)}, f32[8,1024]{1,0:T(8,128)S(1)}) custom-call(bf16[4096,512]{1,0:T(8,128)(2,1)S(1)} %get-tuple-element.26.samples_ref, bf16[32,512]{1,0:T(8,128)(2,1)S(1)} %join.4.refs_0_.first_ref), custom_call_target="tpu_custom_call" | custom-call | flops 1048576 | bytes 2097152 | tf_op jit(solution)/shard_map/prepare/pallas_call | solution.py:60
  11.2 1.3 %collective-permute-done.2.second_ref = bf16[32,512]{1,0:T(8,128)(2,1)S(1)} collective-permute-done((bf16[32,512]{1,0:T(8,128)(2,1)S(1)}, bf16[32,512]{1,0:T(8,128)(2,1)S(1)}, u32[]{:S(2)}, u32[]{:S(2)}) %collective-permute-start.2) | collective-permute-done | bytes 32800 | tf_op jit(solution)/shard_map/ppermute | solution.py:352
  12.5 0.5 %collective-permute-start.3 = (bf16[64,512]{1,0:T(8,128)(2,1)S(1)}, bf16[64,512]{1,0:T(8,128)(2,1)S(1)}, u32[]{:S(2)}, u32[]{:S(2)}) collective-permute-start(bf16[64,512]{1,0:T(8,128)(2,1)S(1)} %join.5.near_ref), channel_id=1, source_target_pairs={{0,1},{1,0},{2,3},{3,2},{4,5},{5,4},{6,7},{7,6},{8,9},{9,8},{10,11... | collective-permute-start | bytes 196616 | tf_op jit(solution)/shard_map/ppermute | solution.py:352
  13.0 0.9 %collective-permute-done.3.far_ref = bf16[64,512]{1,0:T(8,128)(2,1)S(1)} collective-permute-done((bf16[64,512]{1,0:T(8,128)(2,1)S(1)}, bf16[64,512]{1,0:T(8,128)(2,1)S(1)}, u32[]{:S(2)}, u32[]{:S(2)}) %collective-permute-start.3) | collective-permute-done | bytes 65568 | tf_op jit(solution)/shard_map/ppermute | solution.py:352
  13.9 1.8 %cross_terms.1 = (f32[64,640]{1,0:T(8,128)S(1)}, f32[64,640]{1,0:T(8,128)S(1)}) custom-call(bf16[64,512]{1,0:T(8,128)(2,1)S(1)} %join.5.near_ref, bf16[64,512]{1,0:T(8,128)(2,1)S(1)} %collective-permute-done.3.far_ref, bf16[4096,512]{1,0:T(8,128)(2,1)S(1)} %get-tuple-element.26.samples_ref, bf16[512,2048]{1,0:T(8,128)(2,1)S(1)} %get-tuple-element.29.refs_0_, ...), custom_call_target="tpu_custom_call" | custom-call | flops 1073741824 | bytes 8388608 | tf_op jit(solution)/shard_map/cross_terms/pallas_call | solution.py:182
  15.8 0.4 %collective-permute-start.4 = (f32[64,640]{1,0:T(8,128)S(1)}, f32[64,640]{1,0:T(8,128)S(1)}, u32[]{:S(2)}, u32[]{:S(2)}) collective-permute-start(f32[64,640]{1,0:T(8,128)S(1)} %get-tuple-element.33), channel_id=1, source_target_pairs={{0,1},{1,0},{2,3},{3,2},{4,5},{5,4},{6,7},{7,6},{8,9},{9,8},{10,11... | collective-permute-start | bytes 491528 | tf_op jit(solution)/shard_map/ppermute | solution.py:352
  16.2 1.3 %collective-permute-start.5 = (bf16[8,512]{1,0:T(8,128)(2,1)S(1)}, bf16[8,512]{1,0:T(8,128)(2,1)S(1)}, u32[]{:S(2)}, u32[]{:S(2)}) collective-permute-start(bf16[8,512]{1,0:T(8,128)(2,1)S(1)} %get-tuple-element.24.first_ref.own_ref), channel_id=1, source_target_pairs={{0,17},{1,16},{2,19},{3,18},{4,21},{5,20},{6,23},{7,22},{8,25},{9,... | collective-permute-start | bytes 24584 | tf_op jit(solution)/shard_map/ppermute | solution.py:362
  17.5 1.8 %collective-permute-done.5.refs_0_ = bf16[8,512]{1,0:T(8,128)(2,1)S(1)} collective-permute-done((bf16[8,512]{1,0:T(8,128)(2,1)S(1)}, bf16[8,512]{1,0:T(8,128)(2,1)S(1)}, u32[]{:S(2)}, u32[]{:S(2)}) %collective-permute-start.5) | collective-permute-done | bytes 8224 | tf_op jit(solution)/shard_map/ppermute | solution.py:362
  19.3 0.5 %self_terms.1 = (f32[64,512]{1,0:T(8,128)S(1)}, f32[8,640]{1,0:T(8,128)S(1)}, f32[8,640]{1,0:T(8,128)S(1)}) custom-call(bf16[64,512]{1,0:T(8,128)(2,1)S(1)} %join.5.near_ref, bf16[64,512]{1,0:T(8,128)(2,1)S(1)} %collective-permute-done.3.far_ref, bf16[8,512]{1,0:T(8,128)(2,1)S(1)} %collective-permute-done.5.refs_0_), custom_call_target="tpu_custom_call" | custom-call | tf_op jit(solution)/shard_map/self_terms/pallas_call | solution.py:314
  19.8 0.0 collective-permute-done.4.right_ref
  19.8 0.1 combine.3
  19.9 1.3 %collective-permute-start.6 = (bf16[32,640]{1,0:T(8,128)(2,1)S(1)}, bf16[32,640]{1,0:T(8,128)(2,1)S(1)}, u32[]{:S(2)}, u32[]{:S(2)}) collective-permute-start(bf16[32,640]{1,0:T(8,128)(2,1)S(1)} %get-tuple-element.36), channel_id=1, source_target_pairs={{0,3},{1,2},{2,1},{3,0},{4,7},{5,6},{6,5},{7,4},{8,11},{9,10},{10,... | collective-permute-start | bytes 122888 | tf_op jit(solution)/shard_map/ppermute | solution.py:352
  21.3 2.3 %collective-permute-done.6.right_ref = bf16[32,640]{1,0:T(8,128)(2,1)S(1)} collective-permute-done((bf16[32,640]{1,0:T(8,128)(2,1)S(1)}, bf16[32,640]{1,0:T(8,128)(2,1)S(1)}, u32[]{:S(2)}, u32[]{:S(2)}) %collective-permute-start.6) | collective-permute-done | bytes 40992 | tf_op jit(solution)/shard_map/ppermute | solution.py:352
  23.5 0.1 combine.4
  23.6 1.4 %collective-permute-start.7 = (bf16[16,640]{1,0:T(8,128)(2,1)S(1)}, bf16[16,640]{1,0:T(8,128)(2,1)S(1)}, u32[]{:S(2)}, u32[]{:S(2)}) collective-permute-start(bf16[16,640]{1,0:T(8,128)(2,1)S(1)} %get-tuple-element.38), channel_id=1, source_target_pairs={{0,5},{1,4},{2,7},{3,6},{4,1},{5,0},{6,3},{7,2},{8,13},{9,12},{10,... | collective-permute-start | bytes 61448 | tf_op jit(solution)/shard_map/ppermute | solution.py:352
  25.0 1.4 %collective-permute-start.9 = (f32[8,640]{1,0:T(8,128)S(1)}, f32[8,640]{1,0:T(8,128)S(1)}, u32[]{:S(2)}, u32[]{:S(2)}) collective-permute-start(f32[8,640]{1,0:T(8,128)S(1)} %get-tuple-element.42), channel_id=1, source_target_pairs={{0,17},{1,16},{2,19},{3,18},{4,21},{5,20},{6,23},{7,22},{8,25},{9,... | collective-permute-start | bytes 61448 | tf_op jit(solution)/shard_map/ppermute | solution.py:362
  26.5 0.4 %collective-permute-done.7.right_ref = bf16[16,640]{1,0:T(8,128)(2,1)S(1)} collective-permute-done((bf16[16,640]{1,0:T(8,128)(2,1)S(1)}, bf16[16,640]{1,0:T(8,128)(2,1)S(1)}, u32[]{:S(2)}, u32[]{:S(2)}) %collective-permute-start.7) | collective-permute-done | bytes 20512 | tf_op jit(solution)/shard_map/ppermute | solution.py:352
  26.9 0.1 combine.5
  27.0 1.9 %collective-permute-start.8 = (bf16[8,640]{1,0:T(8,128)(2,1)S(1)}, bf16[8,640]{1,0:T(8,128)(2,1)S(1)}, u32[]{:S(2)}, u32[]{:S(2)}) collective-permute-start(bf16[8,640]{1,0:T(8,128)(2,1)S(1)} %get-tuple-element.40), channel_id=1, source_target_pairs={{0,9},{1,8},{2,11},{3,10},{4,13},{5,12},{6,15},{7,14},{8,1},{9,0},... | collective-permute-start | bytes 30728 | tf_op jit(solution)/shard_map/ppermute | solution.py:352
  28.9 0.0 collective-permute-done.9.refs_1_
  28.9 2.1 %collective-permute-done.8.right_ref = bf16[8,640]{1,0:T(8,128)(2,1)S(1)} collective-permute-done((bf16[8,640]{1,0:T(8,128)(2,1)S(1)}, bf16[8,640]{1,0:T(8,128)(2,1)S(1)}, u32[]{:S(2)}, u32[]{:S(2)}) %collective-permute-start.8) | collective-permute-done | bytes 10272 | tf_op jit(solution)/shard_map/ppermute | solution.py:352
  31.1 0.7 %final.1 = f32[8,512]{1,0:T(8,128)} custom-call(bf16[8,512]{1,0:T(8,128)(2,1)S(1)} %get-tuple-element.24.first_ref.own_ref, f32[8,640]{1,0:T(8,128)S(1)} %get-tuple-element.39.left_ref, bf16[8,640]{1,0:T(8,128)(2,1)S(1)} %collective-permute-done.8.right_ref, f32[64,512]{1,0:T(8,128)S(1)} %get-tuple-element.34.centre_ref, ...), custom_call_target="tpu_custom_call" | custom-call | tf_op jit(solution)/shard_map/final/pallas_call | solution.py:340
  (3 shorter events, 0.0 us)
Async XLA Ops:
  0.0 5.8 %collective-permute-start = (bf16[8,512]{1,0:T(8,128)(2,1)}, bf16[8,512]{1,0:T(8,128)(2,1)S(1)}, u32[]{:S(2)}, u32[]{:S(2)}) collective-permute-start(bf16[8,512]{1,0:T(8,128)(2,1)} %own_ref.1), channel_id=1, source_target_pairs={{0,9},{1,8},{2,11},{3,10},{4,13},{5,12},{6,15},{7,14},{8,1},{9,0},... | collective-permute-start | bytes 24584 | tf_op jit(solution)/shard_map/ppermute | solution.py:352
  5.8 3.4 %collective-permute-start.1 = (bf16[16,512]{1,0:T(8,128)(2,1)S(1)}, bf16[16,512]{1,0:T(8,128)(2,1)S(1)}, u32[]{:S(2)}, u32[]{:S(2)}) collective-permute-start(bf16[16,512]{1,0:T(8,128)(2,1)S(1)} %join.3.refs_0_.first_ref), channel_id=1, source_target_pairs={{0,5},{1,4},{2,7},{3,6},{4,1},{5,0},{6,3},{7,2},{8,13},{9,12},{10,... | collective-permute-start | bytes 49160 | tf_op jit(solution)/shard_map/ppermute | solution.py:352
  9.1 3.3 %collective-permute-start.2 = (bf16[32,512]{1,0:T(8,128)(2,1)S(1)}, bf16[32,512]{1,0:T(8,128)(2,1)S(1)}, u32[]{:S(2)}, u32[]{:S(2)}) collective-permute-start(bf16[32,512]{1,0:T(8,128)(2,1)S(1)} %join.4.refs_0_.first_ref), channel_id=1, source_target_pairs={{0,3},{1,2},{2,1},{3,0},{4,7},{5,6},{6,5},{7,4},{8,11},{9,10},{10,... | collective-permute-start | bytes 98312 | tf_op jit(solution)/shard_map/ppermute | solution.py:352
  12.5 1.4 %collective-permute-start.3 = (bf16[64,512]{1,0:T(8,128)(2,1)S(1)}, bf16[64,512]{1,0:T(8,128)(2,1)S(1)}, u32[]{:S(2)}, u32[]{:S(2)}) collective-permute-start(bf16[64,512]{1,0:T(8,128)(2,1)S(1)} %join.5.near_ref), channel_id=1, source_target_pairs={{0,1},{1,0},{2,3},{3,2},{4,5},{5,4},{6,7},{7,6},{8,9},{9,8},{10,11... | collective-permute-start | bytes 196616 | tf_op jit(solution)/shard_map/ppermute | solution.py:352
  15.8 4.0 %collective-permute-start.4 = (f32[64,640]{1,0:T(8,128)S(1)}, f32[64,640]{1,0:T(8,128)S(1)}, u32[]{:S(2)}, u32[]{:S(2)}) collective-permute-start(f32[64,640]{1,0:T(8,128)S(1)} %get-tuple-element.33), channel_id=1, source_target_pairs={{0,1},{1,0},{2,3},{3,2},{4,5},{5,4},{6,7},{7,6},{8,9},{9,8},{10,11... | collective-permute-start | bytes 491528 | tf_op jit(solution)/shard_map/ppermute | solution.py:352
  16.2 3.1 %collective-permute-start.5 = (bf16[8,512]{1,0:T(8,128)(2,1)S(1)}, bf16[8,512]{1,0:T(8,128)(2,1)S(1)}, u32[]{:S(2)}, u32[]{:S(2)}) collective-permute-start(bf16[8,512]{1,0:T(8,128)(2,1)S(1)} %get-tuple-element.24.first_ref.own_ref), channel_id=1, source_target_pairs={{0,17},{1,16},{2,19},{3,18},{4,21},{5,20},{6,23},{7,22},{8,25},{9,... | collective-permute-start | bytes 24584 | tf_op jit(solution)/shard_map/ppermute | solution.py:362
  19.9 3.6 %collective-permute-start.6 = (bf16[32,640]{1,0:T(8,128)(2,1)S(1)}, bf16[32,640]{1,0:T(8,128)(2,1)S(1)}, u32[]{:S(2)}, u32[]{:S(2)}) collective-permute-start(bf16[32,640]{1,0:T(8,128)(2,1)S(1)} %get-tuple-element.36), channel_id=1, source_target_pairs={{0,3},{1,2},{2,1},{3,0},{4,7},{5,6},{6,5},{7,4},{8,11},{9,10},{10,... | collective-permute-start | bytes 122888 | tf_op jit(solution)/shard_map/ppermute | solution.py:352
  23.6 3.3 %collective-permute-start.7 = (bf16[16,640]{1,0:T(8,128)(2,1)S(1)}, bf16[16,640]{1,0:T(8,128)(2,1)S(1)}, u32[]{:S(2)}, u32[]{:S(2)}) collective-permute-start(bf16[16,640]{1,0:T(8,128)(2,1)S(1)} %get-tuple-element.38), channel_id=1, source_target_pairs={{0,5},{1,4},{2,7},{3,6},{4,1},{5,0},{6,3},{7,2},{8,13},{9,12},{10,... | collective-permute-start | bytes 61448 | tf_op jit(solution)/shard_map/ppermute | solution.py:352
  25.0 3.9 %collective-permute-start.9 = (f32[8,640]{1,0:T(8,128)S(1)}, f32[8,640]{1,0:T(8,128)S(1)}, u32[]{:S(2)}, u32[]{:S(2)}) collective-permute-start(f32[8,640]{1,0:T(8,128)S(1)} %get-tuple-element.42), channel_id=1, source_target_pairs={{0,17},{1,16},{2,19},{3,18},{4,21},{5,20},{6,23},{7,22},{8,25},{9,... | collective-permute-start | bytes 61448 | tf_op jit(solution)/shard_map/ppermute | solution.py:362
  27.0 4.1 %collective-permute-start.8 = (bf16[8,640]{1,0:T(8,128)(2,1)S(1)}, bf16[8,640]{1,0:T(8,128)(2,1)S(1)}, u32[]{:S(2)}, u32[]{:S(2)}) collective-permute-start(bf16[8,640]{1,0:T(8,128)(2,1)S(1)} %get-tuple-element.40), channel_id=1, source_target_pairs={{0,9},{1,8},{2,11},{3,10},{4,13},{5,12},{6,15},{7,14},{8,1},{9,0},... | collective-permute-start | bytes 30728 | tf_op jit(solution)/shard_map/ppermute | solution.py:352
where the time goes:
time: 32 us; the launch traced here: 31.8 us
  starting transfers between devices  15.4 us (48%)
  waiting for transfers between devices  9.99 us (31%)
  Pallas kernels  6.29 us (20%)
    ppermute x8, starting transfers between devices, swap(): return lax.ppermute(values, 'ref', [(i, i ^ mask) for i in range(size)])  12.7 us
    ppermute x8, waiting for transfers between devices, swap(): return lax.ppermute(values, 'ref', [(i, i ^ mask) for i in range(size)])  8.16 us
    ppermute x2, starting transfers between devices, across(): return lax.ppermute(values, ('grp', 'ref'), pairs)  2.7 us
    pallas_call x1, Pallas kernels, stage(): pl.pallas_call(stage_kernel, out_shape=(pltpu.VMEM(own.shape, own.dtype),...  2.24 us
    pallas_call x1, Pallas kernels, cross_terms(): pl.pallas_call(cross_kernel, out_shape=(part, part), in_specs=[VMEM] * (3...  1.84 us
    ppermute x2, waiting for transfers between devices, across(): return lax.ppermute(values, ('grp', 'ref'), pairs)  1.82 us
    pallas_call x1, Pallas kernels, final(): pl.pallas_call(final_kernel, out_shape=jax.ShapeDtypeStruct(own.shape, F3...  0.71 us
    pallas_call x2, Pallas kernels, prepare(): pl.pallas_call(functools.partial(prepare_kernel, first), out_shape=(jax.S...  0.69 us
  transfers between devices with their start and end apart: 10, of which 7 were waited for; matrix products, arithmetic and copies ran while one was open for 0% of the time, Pallas kernels for 11%

commit v1 on v0

--- a/solution.py
+++ b/solution.py
@@ -16,6 +16,7 @@
 ANY = pl.BlockSpec(memory_space=pl.ANY)
 HBM = pl.BlockSpec(memory_space=pltpu.HBM)
 SMALL = 2 << 20
+STAGED = 2
 F32 = jnp.float32
 BF16 = jnp.bfloat16
 HALF = 1.0 / (2.0 * KERNEL_WIDTH)
@@ -115,20 +116,20 @@
     )(in_hbm(own), in_hbm(samples))
 
 
-def join_kernel(first_ref, second_ref, *refs):
-    refs[-1][...] = jnp.concatenate([first_ref[...], second_ref[...]], axis=0)
-
-
-def join(first, second, after=()):
-    rows, width = first.shape
-    return pl.pallas_call(
-        join_kernel,
-        out_shape=jax.ShapeDtypeStruct((2 * rows, width), first.dtype),
-        in_specs=[VMEM, VMEM] + [ANY] * len(after),
+def join_kernel(count, *refs):
+    refs[-1][...] = jnp.concatenate([ref[...] for ref in refs[:count]], axis=0)
+
+
+def join(blocks, after=()):
+    rows, width = blocks[0].shape
+    return pl.pallas_call(
+        functools.partial(join_kernel, len(blocks)),
+        out_shape=jax.ShapeDtypeStruct((len(blocks) * rows, width), blocks[0].dtype),
+        in_specs=[VMEM] * len(blocks) + [ANY] * len(after),
         out_specs=VMEM,
         compiler_params=pltpu.CompilerParams(vmem_limit_bytes=SMALL),
         name="join",
-    )(first, second, *after)
+    )(*blocks, *after)
 
 
 def packed(ref, sums, top, total):
@@ -243,41 +244,41 @@
     return sums, top, sum(part[2] * scale for part, scale in zip(parts, scales))
 
 
-def halves(sums, top, total, keep_ref, send_ref):
-    half = keep_ref.shape[0]
+def shared_out(sums, top, total, keep_ref, send_refs):
+    rows = keep_ref.shape[0]
     packed(
         keep_ref,
-        jnp.concatenate([tile[:half] for tile in sums], axis=1),
-        top[:half],
-        total[:half],
+        jnp.concatenate([tile[:rows] for tile in sums], axis=1),
+        top[:rows],
+        total[:rows],
     )
-    parcel(send_ref, [tile[half:] for tile in sums], top[half:], total[half:])
-
-
-def first_combine_kernel(left_ref, right_ref, centre_ref, keep_ref, send_ref):
+    for index, ref in enumerate(send_refs):
+        here = slice((index + 1) * rows, (index + 2) * rows)
+        parcel(ref, [tile[here] for tile in sums], top[here], total[here])
+
+
+def first_combine_kernel(left_ref, right_ref, centre_ref, keep_ref, *send_refs):
     sums, top, total = combined([loaded(left_ref), loaded(right_ref)])
     sums = [
         tile - total * centre_ref[:, pl.ds(index * LANES, LANES)]
         for index, tile in enumerate(sums)
     ]
-    halves(sums, top, total, keep_ref, send_ref)
-
-
-def next_combine_kernel(left_ref, right_ref, keep_ref, send_ref):
-    halves(*combined([loaded(left_ref), opened(right_ref)]), keep_ref, send_ref)
-
-
-def combine(left, right, centres=None):
-    rows, width = left.shape[0] // 2, left.shape[1]
+    shared_out(sums, top, total, keep_ref, send_refs)
+
+
+def next_combine_kernel(left_ref, right_ref, keep_ref, *send_refs):
+    shared_out(*combined([loaded(left_ref), opened(right_ref)]), keep_ref, send_refs)
+
+
+def combine(left, right, sends, centres=None):
+    rows, width = left.shape[0] // (1 + sends), left.shape[1]
     more = () if centres is None else (centres,)
     return pl.pallas_call(
         next_combine_kernel if centres is None else first_combine_kernel,
-        out_shape=(
-            jax.ShapeDtypeStruct((rows, width), F32),
-            jax.ShapeDtypeStruct((rows, width), BF16),
-        ),
+        out_shape=(jax.ShapeDtypeStruct((rows, width), F32),)
+        + (jax.ShapeDtypeStruct((rows, width), BF16),) * sends,
         in_specs=[VMEM] * (2 + len(more)),
-        out_specs=(VMEM, VMEM),
+        out_specs=(VMEM,) * (1 + sends),
         compiler_params=pltpu.CompilerParams(vmem_limit_bytes=SMALL),
         name="combine",
     )(left, right, *more)
@@ -321,10 +322,10 @@
     )(near, far, *visitors)
 
 
-def final_kernel(own_ref, left_ref, right_ref, centre_ref, *refs):
-    self_refs, out_ref = refs[:-1], refs[-1]
+def final_kernel(arrived, own_ref, left_ref, centre_ref, *refs):
+    right_refs, self_refs, out_ref = refs[:arrived], refs[arrived:-1], refs[-1]
     rows = own_ref.shape[0]
-    sums, _, total = combined([loaded(left_ref), opened(right_ref)])
+    sums, _, total = combined([loaded(left_ref)] + [opened(ref) for ref in right_refs])
     self_sums, _, self_total = combined([loaded(ref) for ref in self_refs])
     scale = 1.0 / total
     self_scale = 1.0 / self_total
@@ -336,15 +337,15 @@
         )
 
 
-def final(own, left, right, centres, self_parts):
-    return pl.pallas_call(
-        final_kernel,
+def final(own, left, centres, rights, self_parts):
+    return pl.pallas_call(
+        functools.partial(final_kernel, len(rights)),
         out_shape=jax.ShapeDtypeStruct(own.shape, F32),
-        in_specs=[VMEM] * (4 + len(self_parts)),
+        in_specs=[VMEM] * (3 + len(rights) + len(self_parts)),
         out_specs=VMEM,
         compiler_params=pltpu.CompilerParams(vmem_limit_bytes=SMALL),
         name="final",
-    )(own, left, right, centres, *self_parts)
+    )(own, left, centres, *rights, *self_parts)
 
 
 def swap(values, mask):
@@ -364,37 +365,37 @@
 
 def swap_masks(size):
     count = size.bit_length() - 1
-    assert size == 1 << count and count >= 3
-    return [1] + [(1 << k) | 1 for k in range(1, count)]
+    assert size == 1 << count and count >= 4
+    low, high = 1 << (count - 2), 1 << (count - 1)
+    singles = [1] + [(1 << k) | 1 for k in range(1, count - 2)]
+    return singles, [high | low | 1, low, high | 1]
 
 
 def per_device(particles, samples):
-    ref_size = lax.axis_size("ref")
     grp_size = lax.axis_size("grp")
-    masks = swap_masks(ref_size)
+    singles, triple = swap_masks(lax.axis_size("ref"))
     count = samples.shape[0]
-    half = count // 2
-    own, staged, *first_part = stage(particles, samples, half, 8)
+    own, staged, *first_part = stage(particles, samples, count * STAGED // 4, 8)
     prepared = [first_part]
-    block = own
-    for mask in reversed(masks[1:]):
-        other = swap(particles if block is own else block, mask)
-        if block is not own and len(prepared) < 3:
-            quarter = half // 2
-            prepared.append(
-                prepare(staged, half + (len(prepared) - 1) * quarter, quarter, [block])
-            )
-        block = join(block, other, prepared[-1][1:])
-    far_block = swap(block, masks[0])
+    others = [swap(particles, mask) for mask in triple]
+    block = join([own] + others, first_part[1:])
+    prepared += [
+        prepare(staged, part * count // 4, count // 4, [block]) for part in range(STAGED, 4)
+    ]
+    for mask in reversed(singles[1:]):
+        block = join([block, swap(block, mask)], prepared[-1][1:])
+    far_block = swap(block, singles[0])
     keep, send = cross_terms(block, far_block, staged, prepared)
     visitors = [across(own, k) for k in range(1, grp_size)]
     centres, *self_parts = self_terms(block, far_block, visitors, own.shape[0])
     returned = [across(part, -k) for k, part in zip(range(1, grp_size), self_parts[1:])]
-    keep, send = combine(keep, swap(send, masks[0]), centres)
-    for mask in masks[1:-1]:
-        keep, send = combine(keep, swap(send, mask))
-    last = swap(send, masks[-1])
-    return final(own, keep, last, centres, [self_parts[0]] + returned)
+    sends, more = [send], (centres,)
+    for index, mask in enumerate(singles):
+        count = 1 if index < len(singles) - 1 else len(triple)
+        keep, *sends = combine(keep, swap(sends[0], mask), count, *more)
+        more = ()
+    rights = [swap(part, mask) for part, mask in zip(sends, triple)]
+    return final(own, keep, centres, rights, [self_parts[0]] + returned)
 
 
 def solution(mesh):

time: 32 us -> 30.3 us (0.947)
  waiting for transfers between devices: 9.99 us -> 8.12 us
    ppermute x8 -> x10, waiting for transfers between devices: 8.16 us -> 6.29 us  [swap(): return lax.ppermute(values, 'ref', [(i, i ^ mask) for i in range(size)])]
    ppermute x8 -> x10, starting transfers between devices: 12.7 us -> 13 us  [swap(): return lax.ppermute(values, 'ref', [(i, i ^ mask) for i in range(size)])]
    pallas_call x4 -> x3, Pallas kernels: 0.72 us -> 0.73 us  [the longest x1 0.71 us: final(): pl.pallas_call(functools.partial(final_kernel, len(rights)), out_shape=ja...]
  transfers between devices with their start and end apart: 10 -> 12, of which waited for: 7 -> 9; matrix products, arithmetic and copies ran while one was open for 0% -> 0% of each run, Pallas kernels for 11% -> 12%
where the time goes in v1:
time: 30.3 us; the launch traced here: 30 us
  starting transfers between devices  15.7 us (52%)
  waiting for transfers between devices  8.12 us (27%)
  Pallas kernels  6.2 us (20%)
    ppermute x10, starting transfers between devices, swap(): return lax.ppermute(values, 'ref', [(i, i ^ mask) for i in range(size)])  13 us
    ppermute x10, waiting for transfers between devices, swap(): return lax.ppermute(values, 'ref', [(i, i ^ mask) for i in range(size)])  6.29 us
    ppermute x2, starting transfers between devices, across(): return lax.ppermute(values, ('grp', 'ref'), pairs)  2.7 us
    pallas_call x1, Pallas kernels, stage(): pl.pallas_call(stage_kernel, out_shape=(pltpu.VMEM(own.shape, own.dtype),...  2.24 us
    pallas_call x1, Pallas kernels, cross_terms(): pl.pallas_call(cross_kernel, out_shape=(part, part), in_specs=[VMEM] * (3...  1.84 us
    ppermute x2, waiting for transfers between devices, across(): return lax.ppermute(values, ('grp', 'ref'), pairs)  1.82 us
    pallas_call x1, Pallas kernels, final(): pl.pallas_call(functools.partial(final_kernel, len(rights)), out_shape=ja...  0.71 us
    pallas_call x2, Pallas kernels, prepare(): pl.pallas_call(functools.partial(prepare_kernel, first), out_shape=(jax.S...  0.69 us
  transfers between devices with their start and end apart: 12, of which 9 were waited for; matrix products, arithmetic and copies ran while one was open for 0% of the time, Pallas kernels for 12%

profile of v1, /device:TPU:0, one launch (start us, length us, event | category | flops | bytes accessed | tf_op | source)
XLA Modules:
  0.0 30.0 jit_solution(6963527737794540431)
XLA Ops:
  0.0 4.5 %collective-permute-start = (bf16[8,512]{1,0:T(8,128)(2,1)}, bf16[8,512]{1,0:T(8,128)(2,1)S(1)}, u32[]{:S(2)}, u32[]{:S(2)}) collective-permute-start(bf16[8,512]{1,0:T(8,128)(2,1)} %own_ref.1), channel_id=1, source_target_pairs={{0,13},{1,12},{2,15},{3,14},{4,9},{5,8},{6,11},{7,10},{8,5},{9,4},... | collective-permute-start | bytes 24584 | tf_op jit(solution)/shard_map/ppermute | solution.py:353
  4.5 0.0 collective-permute-start.1
  4.5 0.3 collective-permute-start.2
  4.8 2.2 %stage.1 = (bf16[8,512]{1,0:T(8,128)(2,1)S(1)}, bf16[4096,512]{1,0:T(8,128)(2,1)S(1)}, bf16[512,2048]{1,0:T(8,128)(2,1)S(1)}, f32[8,2048]{1,0:T(8,128)S(1)}) custom-call(bf16[8,512]{1,0:T(8,128)(2,1)} %own_ref.1, bf16[4096,512]{1,0:T(8,128)(2,1)} %samples_ref.1), custom_call_target="tpu_custom_call" | custom-call | tf_op jit(solution)/shard_map/stage/pallas_call | solution.py:103
  7.1 0.0 collective-permute-done.refs_1_
  7.1 1.3 %collective-permute-done.1.refs_2_ = bf16[8,512]{1,0:T(8,128)(2,1)S(1)} collective-permute-done((bf16[8,512]{1,0:T(8,128)(2,1)}, bf16[8,512]{1,0:T(8,128)(2,1)S(1)}, u32[]{:S(2)}, u32[]{:S(2)}) %collective-permute-start.1) | collective-permute-done | bytes 8224 | tf_op jit(solution)/shard_map/ppermute | solution.py:353
  8.4 0.3 %collective-permute-done.2.refs_3_ = bf16[8,512]{1,0:T(8,128)(2,1)S(1)} collective-permute-done((bf16[8,512]{1,0:T(8,128)(2,1)}, bf16[8,512]{1,0:T(8,128)(2,1)S(1)}, u32[]{:S(2)}, u32[]{:S(2)}) %collective-permute-start.2) | collective-permute-done | bytes 8224 | tf_op jit(solution)/shard_map/ppermute | solution.py:353
  8.7 1.9 %collective-permute-start.3 = (bf16[32,512]{1,0:T(8,128)(2,1)S(1)}, bf16[32,512]{1,0:T(8,128)(2,1)S(1)}, u32[]{:S(2)}, u32[]{:S(2)}) collective-permute-start(bf16[32,512]{1,0:T(8,128)(2,1)S(1)} %join.2.refs_0_), channel_id=1, source_target_pairs={{0,3},{1,2},{2,1},{3,0},{4,7},{5,6},{6,5},{7,4},{8,11},{9,10},{10,... | collective-permute-start | bytes 98312 | tf_op jit(solution)/shard_map/ppermute | solution.py:353
  10.6 0.3 %prepare.2 = (bf16[512,1024]{1,0:T(8,128)(2,1)S(1)}, f32[8,1024]{1,0:T(8,128)S(1)}) custom-call(bf16[4096,512]{1,0:T(8,128)(2,1)S(1)} %get-tuple-element.26.samples_ref, bf16[32,512]{1,0:T(8,128)(2,1)S(1)} %join.2.refs_0_), custom_call_target="tpu_custom_call" | custom-call | flops 1048576 | bytes 2097152 | tf_op jit(solution)/shard_map/prepare/pallas_call | solution.py:61
  10.9 1.3 %collective-permute-done.3.refs_1_ = bf16[32,512]{1,0:T(8,128)(2,1)S(1)} collective-permute-done((bf16[32,512]{1,0:T(8,128)(2,1)S(1)}, bf16[32,512]{1,0:T(8,128)(2,1)S(1)}, u32[]{:S(2)}, u32[]{:S(2)}) %collective-permute-start.3) | collective-permute-done | bytes 32800 | tf_op jit(solution)/shard_map/ppermute | solution.py:353
  12.2 0.6 %collective-permute-start.4 = (bf16[64,512]{1,0:T(8,128)(2,1)S(1)}, bf16[64,512]{1,0:T(8,128)(2,1)S(1)}, u32[]{:S(2)}, u32[]{:S(2)}) collective-permute-start(bf16[64,512]{1,0:T(8,128)(2,1)S(1)} %join.3.near_ref), channel_id=1, source_target_pairs={{0,1},{1,0},{2,3},{3,2},{4,5},{5,4},{6,7},{7,6},{8,9},{9,8},{10,11... | collective-permute-start | bytes 196616 | tf_op jit(solution)/shard_map/ppermute | solution.py:353
  12.8 0.3 %prepare.3 = (bf16[512,1024]{1,0:T(8,128)(2,1)S(1)}, f32[8,1024]{1,0:T(8,128)S(1)}) custom-call(bf16[4096,512]{1,0:T(8,128)(2,1)S(1)} %get-tuple-element.26.samples_ref, bf16[32,512]{1,0:T(8,128)(2,1)S(1)} %join.2.refs_0_), custom_call_target="tpu_custom_call" | custom-call | flops 1048576 | bytes 2097152 | tf_op jit(solution)/shard_map/prepare/pallas_call | solution.py:61
  13.2 0.6 %collective-permute-done.4.far_ref = bf16[64,512]{1,0:T(8,128)(2,1)S(1)} collective-permute-done((bf16[64,512]{1,0:T(8,128)(2,1)S(1)}, bf16[64,512]{1,0:T(8,128)(2,1)S(1)}, u32[]{:S(2)}, u32[]{:S(2)}) %collective-permute-start.4) | collective-permute-done | bytes 65568 | tf_op jit(solution)/shard_map/ppermute | solution.py:353
  13.7 1.8 %cross_terms.1 = (f32[64,640]{1,0:T(8,128)S(1)}, f32[64,640]{1,0:T(8,128)S(1)}) custom-call(bf16[64,512]{1,0:T(8,128)(2,1)S(1)} %join.3.near_ref, bf16[64,512]{1,0:T(8,128)(2,1)S(1)} %collective-permute-done.4.far_ref, bf16[4096,512]{1,0:T(8,128)(2,1)S(1)} %get-tuple-element.26.samples_ref, bf16[512,2048]{1,0:T(8,128)(2,1)S(1)} %get-tuple-element.28.refs_0_, ...), custom_call_target="tpu_custom_call" | custom-call | flops 1073741824 | bytes 8388608 | tf_op jit(solution)/shard_map/cross_terms/pallas_call | solution.py:183
  15.6 0.4 %collective-permute-start.5 = (f32[64,640]{1,0:T(8,128)S(1)}, f32[64,640]{1,0:T(8,128)S(1)}, u32[]{:S(2)}, u32[]{:S(2)}) collective-permute-start(f32[64,640]{1,0:T(8,128)S(1)} %get-tuple-element.33), channel_id=1, source_target_pairs={{0,1},{1,0},{2,3},{3,2},{4,5},{5,4},{6,7},{7,6},{8,9},{9,8},{10,11... | collective-permute-start | bytes 491528 | tf_op jit(solution)/shard_map/ppermute | solution.py:353
  16.0 1.3 %collective-permute-start.6 = (bf16[8,512]{1,0:T(8,128)(2,1)S(1)}, bf16[8,512]{1,0:T(8,128)(2,1)S(1)}, u32[]{:S(2)}, u32[]{:S(2)}) collective-permute-start(bf16[8,512]{1,0:T(8,128)(2,1)S(1)} %get-tuple-element.24.refs_0_.own_ref), channel_id=1, source_target_pairs={{0,17},{1,16},{2,19},{3,18},{4,21},{5,20},{6,23},{7,22},{8,25},{9,... | collective-permute-start | bytes 24584 | tf_op jit(solution)/shard_map/ppermute | solution.py:363
  17.2 1.8 %collective-permute-done.6.refs_0_ = bf16[8,512]{1,0:T(8,128)(2,1)S(1)} collective-permute-done((bf16[8,512]{1,0:T(8,128)(2,1)S(1)}, bf16[8,512]{1,0:T(8,128)(2,1)S(1)}, u32[]{:S(2)}, u32[]{:S(2)}) %collective-permute-start.6) | collective-permute-done | bytes 8224 | tf_op jit(solution)/shard_map/ppermute | solution.py:363
  19.1 0.5 %self_terms.1 = (f32[64,512]{1,0:T(8,128)S(1)}, f32[8,640]{1,0:T(8,128)S(1)}, f32[8,640]{1,0:T(8,128)S(1)}) custom-call(bf16[64,512]{1,0:T(8,128)(2,1)S(1)} %join.3.near_ref, bf16[64,512]{1,0:T(8,128)(2,1)S(1)} %collective-permute-done.4.far_ref, bf16[8,512]{1,0:T(8,128)(2,1)S(1)} %collective-permute-done.6.refs_0_), custom_call_target="tpu_custom_call" | custom-call | tf_op jit(solution)/shard_map/self_terms/pallas_call | solution.py:315
  19.5 0.0 collective-permute-done.5.right_ref
  19.5 0.1 combine.2
  19.7 1.4 %collective-permute-start.7 = (bf16[32,640]{1,0:T(8,128)(2,1)S(1)}, bf16[32,640]{1,0:T(8,128)(2,1)S(1)}, u32[]{:S(2)}, u32[]{:S(2)}) collective-permute-start(bf16[32,640]{1,0:T(8,128)(2,1)S(1)} %get-tuple-element.36), channel_id=1, source_target_pairs={{0,3},{1,2},{2,1},{3,0},{4,7},{5,6},{6,5},{7,4},{8,11},{9,10},{10,... | collective-permute-start | bytes 122888 | tf_op jit(solution)/shard_map/ppermute | solution.py:353
  21.0 1.5 %collective-permute-start.11 = (f32[8,640]{1,0:T(8,128)S(1)}, f32[8,640]{1,0:T(8,128)S(1)}, u32[]{:S(2)}, u32[]{:S(2)}) collective-permute-start(f32[8,640]{1,0:T(8,128)S(1)} %get-tuple-element.42), channel_id=1, source_target_pairs={{0,17},{1,16},{2,19},{3,18},{4,21},{5,20},{6,23},{7,22},{8,25},{9,... | collective-permute-start | bytes 61448 | tf_op jit(solution)/shard_map/ppermute | solution.py:363
  22.5 0.8 %collective-permute-done.7.right_ref = bf16[32,640]{1,0:T(8,128)(2,1)S(1)} collective-permute-done((bf16[32,640]{1,0:T(8,128)(2,1)S(1)}, bf16[32,640]{1,0:T(8,128)(2,1)S(1)}, u32[]{:S(2)}, u32[]{:S(2)}) %collective-permute-start.7) | collective-permute-done | bytes 40992 | tf_op jit(solution)/shard_map/ppermute | solution.py:353
  23.3 0.1 combine.3
  23.4 1.9 %collective-permute-start.8 = (bf16[8,640]{1,0:T(8,128)(2,1)S(1)}, bf16[8,640]{1,0:T(8,128)(2,1)S(1)}, u32[]{:S(2)}, u32[]{:S(2)}) collective-permute-start(bf16[8,640]{1,0:T(8,128)(2,1)S(1)} %get-tuple-element.38), channel_id=1, source_target_pairs={{0,13},{1,12},{2,15},{3,14},{4,9},{5,8},{6,11},{7,10},{8,5},{9,4},... | collective-permute-start | bytes 30728 | tf_op jit(solution)/shard_map/ppermute | solution.py:353
  25.3 0.0 collective-permute-start.9
  25.3 1.9 %collective-permute-start.10 = (bf16[8,640]{1,0:T(8,128)(2,1)S(1)}, bf16[8,640]{1,0:T(8,128)(2,1)S(1)}, u32[]{:S(2)}, u32[]{:S(2)}) collective-permute-start(bf16[8,640]{1,0:T(8,128)(2,1)S(1)} %get-tuple-element.40), channel_id=1, source_target_pairs={{0,9},{1,8},{2,11},{3,10},{4,13},{5,12},{6,15},{7,14},{8,1},{9,0},... | collective-permute-start | bytes 30728 | tf_op jit(solution)/shard_map/ppermute | solution.py:353
  27.3 0.0 collective-permute-done.11.refs_4_
  27.3 1.1 %collective-permute-done.8.refs_0_ = bf16[8,640]{1,0:T(8,128)(2,1)S(1)} collective-permute-done((bf16[8,640]{1,0:T(8,128)(2,1)S(1)}, bf16[8,640]{1,0:T(8,128)(2,1)S(1)}, u32[]{:S(2)}, u32[]{:S(2)}) %collective-permute-start.8) | collective-permute-done | bytes 10272 | tf_op jit(solution)/shard_map/ppermute | solution.py:353
  28.3 0.7 %collective-permute-done.9.refs_1_ = bf16[8,640]{1,0:T(8,128)(2,1)S(1)} collective-permute-done((bf16[8,640]{1,0:T(8,128)(2,1)S(1)}, bf16[8,640]{1,0:T(8,128)(2,1)S(1)}, u32[]{:S(2)}, u32[]{:S(2)}) %collective-permute-start.9) | collective-permute-done | bytes 10272 | tf_op jit(solution)/shard_map/ppermute | solution.py:353
  29.0 0.3 %collective-permute-done.10.refs_2_ = bf16[8,640]{1,0:T(8,128)(2,1)S(1)} collective-permute-done((bf16[8,640]{1,0:T(8,128)(2,1)S(1)}, bf16[8,640]{1,0:T(8,128)(2,1)S(1)}, u32[]{:S(2)}, u32[]{:S(2)}) %collective-permute-start.10) | collective-permute-done | bytes 10272 | tf_op jit(solution)/shard_map/ppermute | solution.py:353
  29.3 0.7 %final.1 = f32[8,512]{1,0:T(8,128)} custom-call(bf16[8,512]{1,0:T(8,128)(2,1)S(1)} %get-tuple-element.24.refs_0_.own_ref, f32[8,640]{1,0:T(8,128)S(1)} %get-tuple-element.37.left_ref, f32[64,512]{1,0:T(8,128)S(1)} %get-tuple-element.34.centre_ref, bf16[8,640]{1,0:T(8,128)(2,1)S(1)} %collective-permute-done.8.refs_0_, ...), custom_call_target="tpu_custom_call" | custom-call | tf_op jit(solution)/shard_map/final/pallas_call | solution.py:341
  (2 shorter events, 0.0 us)
Async XLA Ops:
  0.0 7.1 %collective-permute-start = (bf16[8,512]{1,0:T(8,128)(2,1)}, bf16[8,512]{1,0:T(8,128)(2,1)S(1)}, u32[]{:S(2)}, u32[]{:S(2)}) collective-permute-start(bf16[8,512]{1,0:T(8,128)(2,1)} %own_ref.1), channel_id=1, source_target_pairs={{0,13},{1,12},{2,15},{3,14},{4,9},{5,8},{6,11},{7,10},{8,5},{9,4},... | collective-permute-start | bytes 24584 | tf_op jit(solution)/shard_map/ppermute | solution.py:353
  4.5 3.9 %collective-permute-start.1 = (bf16[8,512]{1,0:T(8,128)(2,1)}, bf16[8,512]{1,0:T(8,128)(2,1)S(1)}, u32[]{:S(2)}, u32[]{:S(2)}) collective-permute-start(bf16[8,512]{1,0:T(8,128)(2,1)} %own_ref.1), channel_id=1, source_target_pairs={{0,4},{1,5},{2,6},{3,7},{4,0},{5,1},{6,2},{7,3},{8,12},{9,13},{10,... | collective-permute-start | bytes 24584 | tf_op jit(solution)/shard_map/ppermute | solution.py:353
  4.5 4.2 %collective-permute-start.2 = (bf16[8,512]{1,0:T(8,128)(2,1)}, bf16[8,512]{1,0:T(8,128)(2,1)S(1)}, u32[]{:S(2)}, u32[]{:S(2)}) collective-permute-start(bf16[8,512]{1,0:T(8,128)(2,1)} %own_ref.1), channel_id=1, source_target_pairs={{0,9},{1,8},{2,11},{3,10},{4,13},{5,12},{6,15},{7,14},{8,1},{9,0},... | collective-permute-start | bytes 24584 | tf_op jit(solution)/shard_map/ppermute | solution.py:353
  8.7 3.5 %collective-permute-start.3 = (bf16[32,512]{1,0:T(8,128)(2,1)S(1)}, bf16[32,512]{1,0:T(8,128)(2,1)S(1)}, u32[]{:S(2)}, u32[]{:S(2)}) collective-permute-start(bf16[32,512]{1,0:T(8,128)(2,1)S(1)} %join.2.refs_0_), channel_id=1, source_target_pairs={{0,3},{1,2},{2,1},{3,0},{4,7},{5,6},{6,5},{7,4},{8,11},{9,10},{10,... | collective-permute-start | bytes 98312 | tf_op jit(solution)/shard_map/ppermute | solution.py:353
  12.2 1.5 %collective-permute-start.4 = (bf16[64,512]{1,0:T(8,128)(2,1)S(1)}, bf16[64,512]{1,0:T(8,128)(2,1)S(1)}, u32[]{:S(2)}, u32[]{:S(2)}) collective-permute-start(bf16[64,512]{1,0:T(8,128)(2,1)S(1)} %join.3.near_ref), channel_id=1, source_target_pairs={{0,1},{1,0},{2,3},{3,2},{4,5},{5,4},{6,7},{7,6},{8,9},{9,8},{10,11... | collective-permute-start | bytes 196616 | tf_op jit(solution)/shard_map/ppermute | solution.py:353
  15.6 4.0 %collective-permute-start.5 = (f32[64,640]{1,0:T(8,128)S(1)}, f32[64,640]{1,0:T(8,128)S(1)}, u32[]{:S(2)}, u32[]{:S(2)}) collective-permute-start(f32[64,640]{1,0:T(8,128)S(1)} %get-tuple-element.33), channel_id=1, source_target_pairs={{0,1},{1,0},{2,3},{3,2},{4,5},{5,4},{6,7},{7,6},{8,9},{9,8},{10,11... | collective-permute-start | bytes 491528 | tf_op jit(solution)/shard_map/ppermute | solution.py:353
  16.0 3.1 %collective-permute-start.6 = (bf16[8,512]{1,0:T(8,128)(2,1)S(1)}, bf16[8,512]{1,0:T(8,128)(2,1)S(1)}, u32[]{:S(2)}, u32[]{:S(2)}) collective-permute-start(bf16[8,512]{1,0:T(8,128)(2,1)S(1)} %get-tuple-element.24.refs_0_.own_ref), channel_id=1, source_target_pairs={{0,17},{1,16},{2,19},{3,18},{4,21},{5,20},{6,23},{7,22},{8,25},{9,... | collective-permute-start | bytes 24584 | tf_op jit(solution)/shard_map/ppermute | solution.py:363
  19.7 3.6 %collective-permute-start.7 = (bf16[32,640]{1,0:T(8,128)(2,1)S(1)}, bf16[32,640]{1,0:T(8,128)(2,1)S(1)}, u32[]{:S(2)}, u32[]{:S(2)}) collective-permute-start(bf16[32,640]{1,0:T(8,128)(2,1)S(1)} %get-tuple-element.36), channel_id=1, source_target_pairs={{0,3},{1,2},{2,1},{3,0},{4,7},{5,6},{6,5},{7,4},{8,11},{9,10},{10,... | collective-permute-start | bytes 122888 | tf_op jit(solution)/shard_map/ppermute | solution.py:353
  21.0 6.2 %collective-permute-start.11 = (f32[8,640]{1,0:T(8,128)S(1)}, f32[8,640]{1,0:T(8,128)S(1)}, u32[]{:S(2)}, u32[]{:S(2)}) collective-permute-start(f32[8,640]{1,0:T(8,128)S(1)} %get-tuple-element.42), channel_id=1, source_target_pairs={{0,17},{1,16},{2,19},{3,18},{4,21},{5,20},{6,23},{7,22},{8,25},{9,... | collective-permute-start | bytes 61448 | tf_op jit(solution)/shard_map/ppermute | solution.py:363
  23.4 5.0 %collective-permute-start.8 = (bf16[8,640]{1,0:T(8,128)(2,1)S(1)}, bf16[8,640]{1,0:T(8,128)(2,1)S(1)}, u32[]{:S(2)}, u32[]{:S(2)}) collective-permute-start(bf16[8,640]{1,0:T(8,128)(2,1)S(1)} %get-tuple-element.38), channel_id=1, source_target_pairs={{0,13},{1,12},{2,15},{3,14},{4,9},{5,8},{6,11},{7,10},{8,5},{9,4},... | collective-permute-start | bytes 30728 | tf_op jit(solution)/shard_map/ppermute | solution.py:353
  25.3 3.7 %collective-permute-start.9 = (bf16[8,640]{1,0:T(8,128)(2,1)S(1)}, bf16[8,640]{1,0:T(8,128)(2,1)S(1)}, u32[]{:S(2)}, u32[]{:S(2)}) collective-permute-start(bf16[8,640]{1,0:T(8,128)(2,1)S(1)} %get-tuple-element.39), channel_id=1, source_target_pairs={{0,4},{1,5},{2,6},{3,7},{4,0},{5,1},{6,2},{7,3},{8,12},{9,13},{10,... | collective-permute-start | bytes 30728 | tf_op jit(solution)/shard_map/ppermute | solution.py:353
  25.3 4.0 %collective-permute-start.10 = (bf16[8,640]{1,0:T(8,128)(2,1)S(1)}, bf16[8,640]{1,0:T(8,128)(2,1)S(1)}, u32[]{:S(2)}, u32[]{:S(2)}) collective-permute-start(bf16[8,640]{1,0:T(8,128)(2,1)S(1)} %get-tuple-element.40), channel_id=1, source_target_pairs={{0,9},{1,8},{2,11},{3,10},{4,13},{5,12},{6,15},{7,14},{8,1},{9,0},... | collective-permute-start | bytes 30728 | tf_op jit(solution)/shard_map/ppermute | solution.py:353

commit v2 on v1

--- a/solution.py
+++ b/solution.py
@@ -116,14 +116,18 @@
     )(in_hbm(own), in_hbm(samples))
 
 
-def join_kernel(count, *refs):
-    refs[-1][...] = jnp.concatenate([ref[...] for ref in refs[:count]], axis=0)
-
-
-def join(blocks, after=()):
+def join_kernel(count, runs, *refs):
+    blocks = [ref[...] for ref in refs[:count]]
+    size = blocks[0].shape[0] // runs
+    refs[-1][...] = jnp.concatenate(
+        [block[run * size : (run + 1) * size] for run in range(runs) for block in blocks], axis=0
+    )
+
+
+def join(blocks, runs, after=()):
     rows, width = blocks[0].shape
     return pl.pallas_call(
-        functools.partial(join_kernel, len(blocks)),
+        functools.partial(join_kernel, len(blocks), runs),
         out_shape=jax.ShapeDtypeStruct((len(blocks) * rows, width), blocks[0].dtype),
         in_specs=[VMEM] * len(blocks) + [ANY] * len(after),
         out_specs=VMEM,
@@ -266,22 +270,26 @@
     shared_out(sums, top, total, keep_ref, send_refs)
 
 
-def next_combine_kernel(left_ref, right_ref, keep_ref, *send_refs):
-    shared_out(*combined([loaded(left_ref), opened(right_ref)]), keep_ref, send_refs)
-
-
-def combine(left, right, sends, centres=None):
+def next_combine_kernel(arrived, left_ref, *refs):
+    right_refs, keep_ref, send_refs = refs[:arrived], refs[arrived], refs[arrived + 1 :]
+    parts = [loaded(left_ref)] + [opened(ref) for ref in right_refs]
+    shared_out(*combined(parts), keep_ref, send_refs)
+
+
+def combine(left, rights, sends, centres=None):
     rows, width = left.shape[0] // (1 + sends), left.shape[1]
     more = () if centres is None else (centres,)
     return pl.pallas_call(
-        next_combine_kernel if centres is None else first_combine_kernel,
+        functools.partial(next_combine_kernel, len(rights))
+        if centres is None
+        else first_combine_kernel,
         out_shape=(jax.ShapeDtypeStruct((rows, width), F32),)
         + (jax.ShapeDtypeStruct((rows, width), BF16),) * sends,
-        in_specs=[VMEM] * (2 + len(more)),
+        in_specs=[VMEM] * (1 + len(rights) + len(more)),
         out_specs=(VMEM,) * (1 + sends),
         compiler_params=pltpu.CompilerParams(vmem_limit_bytes=SMALL),
         name="combine",
-    )(left, right, *more)
+    )(left, *rights, *more)
 
 
 def self_kernel(near_ref, far_ref, *refs):
@@ -378,23 +386,22 @@
     own, staged, *first_part = stage(particles, samples, count * STAGED // 4, 8)
     prepared = [first_part]
     others = [swap(particles, mask) for mask in triple]
-    block = join([own] + others, first_part[1:])
+    block = join([own] + others, 1, first_part[1:])
     prepared += [
         prepare(staged, part * count // 4, count // 4, [block]) for part in range(STAGED, 4)
     ]
     for mask in reversed(singles[1:]):
-        block = join([block, swap(block, mask)], prepared[-1][1:])
+        block = join([block, swap(block, mask)], 1 + len(triple), prepared[-1][1:])
     far_block = swap(block, singles[0])
     keep, send = cross_terms(block, far_block, staged, prepared)
     visitors = [across(own, k) for k in range(1, grp_size)]
     centres, *self_parts = self_terms(block, far_block, visitors, own.shape[0])
     returned = [across(part, -k) for k, part in zip(range(1, grp_size), self_parts[1:])]
-    sends, more = [send], (centres,)
-    for index, mask in enumerate(singles):
-        count = 1 if index < len(singles) - 1 else len(triple)
-        keep, *sends = combine(keep, swap(sends[0], mask), count, *more)
-        more = ()
+    keep, *sends = combine(keep, [swap(send, singles[0])], len(triple), centres)
     rights = [swap(part, mask) for part, mask in zip(sends, triple)]
+    for mask in singles[1:]:
+        keep, send = combine(keep, rights, 1)
+        rights = [swap(send, mask)]
     return final(own, keep, centres, rights, [self_parts[0]] + returned)
 
 

time: 30.3 us -> 30.1 us (level)
  waiting for transfers between devices: 8.12 us -> 7.8 us
    ppermute x10, waiting for transfers between devices: 6.29 us -> 5.98 us  [swap(): return lax.ppermute(values, 'ref', [(i, i ^ mask) for i in range(size)])]
  transfers between devices with their start and end apart: 12 -> 12, of which waited for: 9 -> 8; matrix products, arithmetic and copies ran while one was open for 0% -> 0% of each run, Pallas kernels for 12% -> 12%
where the time goes in v2:
time: 30.1 us; the launch traced here: 29.9 us
  starting transfers between devices  15.8 us (52%)
  waiting for transfers between devices  7.8 us (26%)
  Pallas kernels  6.21 us (21%)
    ppermute x10, starting transfers between devices, swap(): return lax.ppermute(values, 'ref', [(i, i ^ mask) for i in range(size)])  13 us
    ppermute x10, waiting for transfers between devices, swap(): return lax.ppermute(values, 'ref', [(i, i ^ mask) for i in range(size)])  5.98 us
    ppermute x2, starting transfers between devices, across(): return lax.ppermute(values, ('grp', 'ref'), pairs)  2.8 us
    pallas_call x1, Pallas kernels, stage(): pl.pallas_call(stage_kernel, out_shape=(pltpu.VMEM(own.shape, own.dtype),...  2.24 us
    pallas_call x1, Pallas kernels, cross_terms(): pl.pallas_call(cross_kernel, out_shape=(part, part), in_specs=[VMEM] * (3...  1.84 us
    ppermute x2, waiting for transfers between devices, across(): return lax.ppermute(values, ('grp', 'ref'), pairs)  1.82 us
    pallas_call x1, Pallas kernels, final(): pl.pallas_call(functools.partial(final_kernel, len(rights)), out_shape=ja...  0.71 us
    pallas_call x2, Pallas kernels, prepare(): pl.pallas_call(functools.partial(prepare_kernel, first), out_shape=(jax.S...  0.69 us
  transfers between devices with their start and end apart: 12, of which 8 were waited for; matrix products, arithmetic and copies ran while one was open for 0% of the time, Pallas kernels for 12%

profile of v2, /device:TPU:0, one launch (start us, length us, event | category | flops | bytes accessed | tf_op | source)
XLA Modules:
  0.0 29.9 jit_solution(9952574089172159671)
XLA Ops:
  0.0 4.5 %collective-permute-start = (bf16[8,512]{1,0:T(8,128)(2,1)}, bf16[8,512]{1,0:T(8,128)(2,1)S(1)}, u32[]{:S(2)}, u32[]{:S(2)}) collective-permute-start(bf16[8,512]{1,0:T(8,128)(2,1)} %own_ref.1), channel_id=1, source_target_pairs={{0,13},{1,12},{2,15},{3,14},{4,9},{5,8},{6,11},{7,10},{8,5},{9,4},... | collective-permute-start | bytes 24584 | tf_op jit(solution)/shard_map/ppermute | solution.py:361
  4.5 0.0 collective-permute-start.1
  4.5 0.3 collective-permute-start.2
  4.8 2.2 %stage.1 = (bf16[8,512]{1,0:T(8,128)(2,1)S(1)}, bf16[4096,512]{1,0:T(8,128)(2,1)S(1)}, bf16[512,2048]{1,0:T(8,128)(2,1)S(1)}, f32[8,2048]{1,0:T(8,128)S(1)}) custom-call(bf16[8,512]{1,0:T(8,128)(2,1)} %own_ref.1, bf16[4096,512]{1,0:T(8,128)(2,1)} %samples_ref.1), custom_call_target="tpu_custom_call" | custom-call | tf_op jit(solution)/shard_map/stage/pallas_call | solution.py:103
  7.1 0.0 collective-permute-done.refs_1_
  7.1 1.3 %collective-permute-done.1.refs_2_ = bf16[8,512]{1,0:T(8,128)(2,1)S(1)} collective-permute-done((bf16[8,512]{1,0:T(8,128)(2,1)}, bf16[8,512]{1,0:T(8,128)(2,1)S(1)}, u32[]{:S(2)}, u32[]{:S(2)}) %collective-permute-start.1) | collective-permute-done | bytes 8224 | tf_op jit(solution)/shard_map/ppermute | solution.py:361
  8.4 0.3 %collective-permute-done.2.refs_3_ = bf16[8,512]{1,0:T(8,128)(2,1)S(1)} collective-permute-done((bf16[8,512]{1,0:T(8,128)(2,1)}, bf16[8,512]{1,0:T(8,128)(2,1)S(1)}, u32[]{:S(2)}, u32[]{:S(2)}) %collective-permute-start.2) | collective-permute-done | bytes 8224 | tf_op jit(solution)/shard_map/ppermute | solution.py:361
  8.7 1.9 %collective-permute-start.3 = (bf16[32,512]{1,0:T(8,128)(2,1)S(1)}, bf16[32,512]{1,0:T(8,128)(2,1)S(1)}, u32[]{:S(2)}, u32[]{:S(2)}) collective-permute-start(bf16[32,512]{1,0:T(8,128)(2,1)S(1)} %join.2.refs_0_), channel_id=1, source_target_pairs={{0,3},{1,2},{2,1},{3,0},{4,7},{5,6},{6,5},{7,4},{8,11},{9,10},{10,... | collective-permute-start | bytes 98312 | tf_op jit(solution)/shard_map/ppermute | solution.py:361
  10.6 0.3 %prepare.2 = (bf16[512,1024]{1,0:T(8,128)(2,1)S(1)}, f32[8,1024]{1,0:T(8,128)S(1)}) custom-call(bf16[4096,512]{1,0:T(8,128)(2,1)S(1)} %get-tuple-element.26.samples_ref, bf16[32,512]{1,0:T(8,128)(2,1)S(1)} %join.2.refs_0_), custom_call_target="tpu_custom_call" | custom-call | flops 1048576 | bytes 2097152 | tf_op jit(solution)/shard_map/prepare/pallas_call | solution.py:61
  10.9 1.3 %collective-permute-done.3.refs_1_ = bf16[32,512]{1,0:T(8,128)(2,1)S(1)} collective-permute-done((bf16[32,512]{1,0:T(8,128)(2,1)S(1)}, bf16[32,512]{1,0:T(8,128)(2,1)S(1)}, u32[]{:S(2)}, u32[]{:S(2)}) %collective-permute-start.3) | collective-permute-done | bytes 32800 | tf_op jit(solution)/shard_map/ppermute | solution.py:361
  12.2 0.7 %collective-permute-start.4 = (bf16[64,512]{1,0:T(8,128)(2,1)S(1)}, bf16[64,512]{1,0:T(8,128)(2,1)S(1)}, u32[]{:S(2)}, u32[]{:S(2)}) collective-permute-start(bf16[64,512]{1,0:T(8,128)(2,1)S(1)} %join.3.near_ref), channel_id=1, source_target_pairs={{0,1},{1,0},{2,3},{3,2},{4,5},{5,4},{6,7},{7,6},{8,9},{9,8},{10,11... | collective-permute-start | bytes 196616 | tf_op jit(solution)/shard_map/ppermute | solution.py:361
  12.9 0.3 %prepare.3 = (bf16[512,1024]{1,0:T(8,128)(2,1)S(1)}, f32[8,1024]{1,0:T(8,128)S(1)}) custom-call(bf16[4096,512]{1,0:T(8,128)(2,1)S(1)} %get-tuple-element.26.samples_ref, bf16[32,512]{1,0:T(8,128)(2,1)S(1)} %join.2.refs_0_), custom_call_target="tpu_custom_call" | custom-call | flops 1048576 | bytes 2097152 | tf_op jit(solution)/shard_map/prepare/pallas_call | solution.py:61
  13.2 0.6 %collective-permute-done.4.far_ref = bf16[64,512]{1,0:T(8,128)(2,1)S(1)} collective-permute-done((bf16[64,512]{1,0:T(8,128)(2,1)S(1)}, bf16[64,512]{1,0:T(8,128)(2,1)S(1)}, u32[]{:S(2)}, u32[]{:S(2)}) %collective-permute-start.4) | collective-permute-done | bytes 65568 | tf_op jit(solution)/shard_map/ppermute | solution.py:361
  13.8 1.8 %cross_terms.1 = (f32[64,640]{1,0:T(8,128)S(1)}, f32[64,640]{1,0:T(8,128)S(1)}) custom-call(bf16[64,512]{1,0:T(8,128)(2,1)S(1)} %join.3.near_ref, bf16[64,512]{1,0:T(8,128)(2,1)S(1)} %collective-permute-done.4.far_ref, bf16[4096,512]{1,0:T(8,128)(2,1)S(1)} %get-tuple-element.26.samples_ref, bf16[512,2048]{1,0:T(8,128)(2,1)S(1)} %get-tuple-element.28.refs_0_, ...), custom_call_target="tpu_custom_call" | custom-call | flops 1073741824 | bytes 8388608 | tf_op jit(solution)/shard_map/cross_terms/pallas_call | solution.py:187
  15.6 0.4 %collective-permute-start.5 = (f32[64,640]{1,0:T(8,128)S(1)}, f32[64,640]{1,0:T(8,128)S(1)}, u32[]{:S(2)}, u32[]{:S(2)}) collective-permute-start(f32[64,640]{1,0:T(8,128)S(1)} %get-tuple-element.33), channel_id=1, source_target_pairs={{0,1},{1,0},{2,3},{3,2},{4,5},{5,4},{6,7},{7,6},{8,9},{9,8},{10,11... | collective-permute-start | bytes 491528 | tf_op jit(solution)/shard_map/ppermute | solution.py:361
  16.1 1.3 %collective-permute-start.6 = (bf16[8,512]{1,0:T(8,128)(2,1)S(1)}, bf16[8,512]{1,0:T(8,128)(2,1)S(1)}, u32[]{:S(2)}, u32[]{:S(2)}) collective-permute-start(bf16[8,512]{1,0:T(8,128)(2,1)S(1)} %get-tuple-element.24.refs_0_.own_ref), channel_id=1, source_target_pairs={{0,17},{1,16},{2,19},{3,18},{4,21},{5,20},{6,23},{7,22},{8,25},{9,... | collective-permute-start | bytes 24584 | tf_op jit(solution)/shard_map/ppermute | solution.py:371
  17.3 1.8 %collective-permute-done.6.refs_0_ = bf16[8,512]{1,0:T(8,128)(2,1)S(1)} collective-permute-done((bf16[8,512]{1,0:T(8,128)(2,1)S(1)}, bf16[8,512]{1,0:T(8,128)(2,1)S(1)}, u32[]{:S(2)}, u32[]{:S(2)}) %collective-permute-start.6) | collective-permute-done | bytes 8224 | tf_op jit(solution)/shard_map/ppermute | solution.py:371
  19.1 0.5 %self_terms.1 = (f32[64,512]{1,0:T(8,128)S(1)}, f32[8,640]{1,0:T(8,128)S(1)}, f32[8,640]{1,0:T(8,128)S(1)}) custom-call(bf16[64,512]{1,0:T(8,128)(2,1)S(1)} %join.3.near_ref, bf16[64,512]{1,0:T(8,128)(2,1)S(1)} %collective-permute-done.4.far_ref, bf16[8,512]{1,0:T(8,128)(2,1)S(1)} %collective-permute-done.6.refs_0_), custom_call_target="tpu_custom_call" | custom-call | tf_op jit(solution)/shard_map/self_terms/pallas_call | solution.py:323
  19.6 0.0 collective-permute-done.5.right_ref
  19.6 0.1 combine.2
  19.8 2.0 %collective-permute-start.7 = (bf16[16,640]{1,0:T(8,128)(2,1)S(1)}, bf16[16,640]{1,0:T(8,128)(2,1)S(1)}, u32[]{:S(2)}, u32[]{:S(2)}) collective-permute-start(bf16[16,640]{1,0:T(8,128)(2,1)S(1)} %get-tuple-element.36), channel_id=1, source_target_pairs={{0,13},{1,12},{2,15},{3,14},{4,9},{5,8},{6,11},{7,10},{8,5},{9,4},... | collective-permute-start | bytes 61448 | tf_op jit(solution)/shard_map/ppermute | solution.py:361
  21.8 0.0 collective-permute-start.8
  21.8 1.8 %collective-permute-start.9 = (bf16[16,640]{1,0:T(8,128)(2,1)S(1)}, bf16[16,640]{1,0:T(8,128)(2,1)S(1)}, u32[]{:S(2)}, u32[]{:S(2)}) collective-permute-start(bf16[16,640]{1,0:T(8,128)(2,1)S(1)} %get-tuple-element.38), channel_id=1, source_target_pairs={{0,9},{1,8},{2,11},{3,10},{4,13},{5,12},{6,15},{7,14},{8,1},{9,0},... | collective-permute-start | bytes 61448 | tf_op jit(solution)/shard_map/ppermute | solution.py:361
  23.7 1.5 %collective-permute-start.11 = (f32[8,640]{1,0:T(8,128)S(1)}, f32[8,640]{1,0:T(8,128)S(1)}, u32[]{:S(2)}, u32[]{:S(2)}) collective-permute-start(f32[8,640]{1,0:T(8,128)S(1)} %get-tuple-element.42), channel_id=1, source_target_pairs={{0,17},{1,16},{2,19},{3,18},{4,21},{5,20},{6,23},{7,22},{8,25},{9,... | collective-permute-start | bytes 61448 | tf_op jit(solution)/shard_map/ppermute | solution.py:371
  25.2 0.0 collective-permute-done.7.refs_0_
  25.2 0.4 %collective-permute-done.8.refs_1_ = bf16[16,640]{1,0:T(8,128)(2,1)S(1)} collective-permute-done((bf16[16,640]{1,0:T(8,128)(2,1)S(1)}, bf16[16,640]{1,0:T(8,128)(2,1)S(1)}, u32[]{:S(2)}, u32[]{:S(2)}) %collective-permute-start.8) | collective-permute-done | bytes 20512 | tf_op jit(solution)/shard_map/ppermute | solution.py:361
  25.6 0.3 %collective-permute-done.9.refs_2_ = bf16[16,640]{1,0:T(8,128)(2,1)S(1)} collective-permute-done((bf16[16,640]{1,0:T(8,128)(2,1)S(1)}, bf16[16,640]{1,0:T(8,128)(2,1)S(1)}, u32[]{:S(2)}, u32[]{:S(2)}) %collective-permute-start.9) | collective-permute-done | bytes 20512 | tf_op jit(solution)/shard_map/ppermute | solution.py:361
  25.9 0.1 combine.3
  26.0 1.4 %collective-permute-start.10 = (bf16[8,640]{1,0:T(8,128)(2,1)S(1)}, bf16[8,640]{1,0:T(8,128)(2,1)S(1)}, u32[]{:S(2)}, u32[]{:S(2)}) collective-permute-start(bf16[8,640]{1,0:T(8,128)(2,1)S(1)} %get-tuple-element.40), channel_id=1, source_target_pairs={{0,3},{1,2},{2,1},{3,0},{4,7},{5,6},{6,5},{7,4},{8,11},{9,10},{10,... | collective-permute-start | bytes 30728 | tf_op jit(solution)/shard_map/ppermute | solution.py:361
  27.4 0.0 collective-permute-done.11.refs_2_
  27.4 1.8 %collective-permute-done.10.refs_0_ = bf16[8,640]{1,0:T(8,128)(2,1)S(1)} collective-permute-done((bf16[8,640]{1,0:T(8,128)(2,1)S(1)}, bf16[8,640]{1,0:T(8,128)(2,1)S(1)}, u32[]{:S(2)}, u32[]{:S(2)}) %collective-permute-start.10) | collective-permute-done | bytes 10272 | tf_op jit(solution)/shard_map/ppermute | solution.py:361
  29.2 0.7 %final.1 = f32[8,512]{1,0:T(8,128)} custom-call(bf16[8,512]{1,0:T(8,128)(2,1)S(1)} %get-tuple-element.24.refs_0_.own_ref, f32[8,640]{1,0:T(8,128)S(1)} %get-tuple-element.39.left_ref, f32[64,512]{1,0:T(8,128)S(1)} %get-tuple-element.34.centre_ref, bf16[8,640]{1,0:T(8,128)(2,1)S(1)} %collective-permute-done.10.refs_0_, ...), custom_call_target="tpu_custom_call" | custom-call | tf_op jit(solution)/shard_map/final/pallas_call | solution.py:349
  (2 shorter events, 0.0 us)
Async XLA Ops:
  0.0 7.1 %collective-permute-start = (bf16[8,512]{1,0:T(8,128)(2,1)}, bf16[8,512]{1,0:T(8,128)(2,1)S(1)}, u32[]{:S(2)}, u32[]{:S(2)}) collective-permute-start(bf16[8,512]{1,0:T(8,128)(2,1)} %own_ref.1), channel_id=1, source_target_pairs={{0,13},{1,12},{2,15},{3,14},{4,9},{5,8},{6,11},{7,10},{8,5},{9,4},... | collective-permute-start | bytes 24584 | tf_op jit(solution)/shard_map/ppermute | solution.py:361
  4.5 3.9 %collective-permute-start.1 = (bf16[8,512]{1,0:T(8,128)(2,1)}, bf16[8,512]{1,0:T(8,128)(2,1)S(1)}, u32[]{:S(2)}, u32[]{:S(2)}) collective-permute-start(bf16[8,512]{1,0:T(8,128)(2,1)} %own_ref.1), channel_id=1, source_target_pairs={{0,4},{1,5},{2,6},{3,7},{4,0},{5,1},{6,2},{7,3},{8,12},{9,13},{10,... | collective-permute-start | bytes 24584 | tf_op jit(solution)/shard_map/ppermute | solution.py:361
  4.5 4.2 %collective-permute-start.2 = (bf16[8,512]{1,0:T(8,128)(2,1)}, bf16[8,512]{1,0:T(8,128)(2,1)S(1)}, u32[]{:S(2)}, u32[]{:S(2)}) collective-permute-start(bf16[8,512]{1,0:T(8,128)(2,1)} %own_ref.1), channel_id=1, source_target_pairs={{0,9},{1,8},{2,11},{3,10},{4,13},{5,12},{6,15},{7,14},{8,1},{9,0},... | collective-permute-start | bytes 24584 | tf_op jit(solution)/shard_map/ppermute | solution.py:361
  8.7 3.5 %collective-permute-start.3 = (bf16[32,512]{1,0:T(8,128)(2,1)S(1)}, bf16[32,512]{1,0:T(8,128)(2,1)S(1)}, u32[]{:S(2)}, u32[]{:S(2)}) collective-permute-start(bf16[32,512]{1,0:T(8,128)(2,1)S(1)} %join.2.refs_0_), channel_id=1, source_target_pairs={{0,3},{1,2},{2,1},{3,0},{4,7},{5,6},{6,5},{7,4},{8,11},{9,10},{10,... | collective-permute-start | bytes 98312 | tf_op jit(solution)/shard_map/ppermute | solution.py:361
  12.2 1.6 %collective-permute-start.4 = (bf16[64,512]{1,0:T(8,128)(2,1)S(1)}, bf16[64,512]{1,0:T(8,128)(2,1)S(1)}, u32[]{:S(2)}, u32[]{:S(2)}) collective-permute-start(bf16[64,512]{1,0:T(8,128)(2,1)S(1)} %join.3.near_ref), channel_id=1, source_target_pairs={{0,1},{1,0},{2,3},{3,2},{4,5},{5,4},{6,7},{7,6},{8,9},{9,8},{10,11... | collective-permute-start | bytes 196616 | tf_op jit(solution)/shard_map/ppermute | solution.py:361
  15.6 4.0 %collective-permute-start.5 = (f32[64,640]{1,0:T(8,128)S(1)}, f32[64,640]{1,0:T(8,128)S(1)}, u32[]{:S(2)}, u32[]{:S(2)}) collective-permute-start(f32[64,640]{1,0:T(8,128)S(1)} %get-tuple-element.33), channel_id=1, source_target_pairs={{0,1},{1,0},{2,3},{3,2},{4,5},{5,4},{6,7},{7,6},{8,9},{9,8},{10,11... | collective-permute-start | bytes 491528 | tf_op jit(solution)/shard_map/ppermute | solution.py:361
  16.1 3.1 %collective-permute-start.6 = (bf16[8,512]{1,0:T(8,128)(2,1)S(1)}, bf16[8,512]{1,0:T(8,128)(2,1)S(1)}, u32[]{:S(2)}, u32[]{:S(2)}) collective-permute-start(bf16[8,512]{1,0:T(8,128)(2,1)S(1)} %get-tuple-element.24.refs_0_.own_ref), channel_id=1, source_target_pairs={{0,17},{1,16},{2,19},{3,18},{4,21},{5,20},{6,23},{7,22},{8,25},{9,... | collective-permute-start | bytes 24584 | tf_op jit(solution)/shard_map/ppermute | solution.py:371
  19.8 5.4 %collective-permute-start.7 = (bf16[16,640]{1,0:T(8,128)(2,1)S(1)}, bf16[16,640]{1,0:T(8,128)(2,1)S(1)}, u32[]{:S(2)}, u32[]{:S(2)}) collective-permute-start(bf16[16,640]{1,0:T(8,128)(2,1)S(1)} %get-tuple-element.36), channel_id=1, source_target_pairs={{0,13},{1,12},{2,15},{3,14},{4,9},{5,8},{6,11},{7,10},{8,5},{9,4},... | collective-permute-start | bytes 61448 | tf_op jit(solution)/shard_map/ppermute | solution.py:361
  21.8 3.8 %collective-permute-start.8 = (bf16[16,640]{1,0:T(8,128)(2,1)S(1)}, bf16[16,640]{1,0:T(8,128)(2,1)S(1)}, u32[]{:S(2)}, u32[]{:S(2)}) collective-permute-start(bf16[16,640]{1,0:T(8,128)(2,1)S(1)} %get-tuple-element.37), channel_id=1, source_target_pairs={{0,4},{1,5},{2,6},{3,7},{4,0},{5,1},{6,2},{7,3},{8,12},{9,13},{10,... | collective-permute-start | bytes 61448 | tf_op jit(solution)/shard_map/ppermute | solution.py:361
  21.8 4.1 %collective-permute-start.9 = (bf16[16,640]{1,0:T(8,128)(2,1)S(1)}, bf16[16,640]{1,0:T(8,128)(2,1)S(1)}, u32[]{:S(2)}, u32[]{:S(2)}) collective-permute-start(bf16[16,640]{1,0:T(8,128)(2,1)S(1)} %get-tuple-element.38), channel_id=1, source_target_pairs={{0,9},{1,8},{2,11},{3,10},{4,13},{5,12},{6,15},{7,14},{8,1},{9,0},... | collective-permute-start | bytes 61448 | tf_op jit(solution)/shard_map/ppermute | solution.py:361
  23.7 3.7 %collective-permute-start.11 = (f32[8,640]{1,0:T(8,128)S(1)}, f32[8,640]{1,0:T(8,128)S(1)}, u32[]{:S(2)}, u32[]{:S(2)}) collective-permute-start(f32[8,640]{1,0:T(8,128)S(1)} %get-tuple-element.42), channel_id=1, source_target_pairs={{0,17},{1,16},{2,19},{3,18},{4,21},{5,20},{6,23},{7,22},{8,25},{9,... | collective-permute-start | bytes 61448 | tf_op jit(solution)/shard_map/ppermute | solution.py:371
  26.0 3.2 %collective-permute-start.10 = (bf16[8,640]{1,0:T(8,128)(2,1)S(1)}, bf16[8,640]{1,0:T(8,128)(2,1)S(1)}, u32[]{:S(2)}, u32[]{:S(2)}) collective-permute-start(bf16[8,640]{1,0:T(8,128)(2,1)S(1)} %get-tuple-element.40), channel_id=1, source_target_pairs={{0,3},{1,2},{2,1},{3,0},{4,7},{5,6},{6,5},{7,4},{8,11},{9,10},{10,... | collective-permute-start | bytes 30728 | tf_op jit(solution)/shard_map/ppermute | solution.py:361

commit v3 on v2

--- a/solution.py
+++ b/solution.py
@@ -143,10 +143,21 @@
     ref[:, width : width + LANES] = jnp.where(lane_id < LANES // 2, top, total)
 
 
-def cross_kernel(near_ref, far_ref, samples_ref, *refs):
+def regrouped(near, far, picks):
+    size = near.shape[0] // len(picks)
+    runs = [
+        [block[run * size : (run + 1) * size] for run in range(len(picks))] for block in (near, far)
+    ]
+    return jnp.concatenate(
+        [runs[side][run] for side, run in picks] + [runs[1 - side][run] for side, run in picks],
+        axis=0,
+    )
+
+
+def cross_kernel(picks, near_ref, far_ref, samples_ref, *refs):
     near_out, far_out = refs[-2:]
     turned_refs, norm_refs = refs[0:-2:2], refs[1:-2:2]
-    group = jnp.concatenate([near_ref[...], far_ref[...]], axis=0)
+    group = regrouped(near_ref[...], far_ref[...], picks)
     rows, _ = group.shape
     wide = group.astype(F32)
     group_sq = jnp.sum(wide * wide, axis=1, keepdims=True) * HALF
@@ -180,12 +191,12 @@
     packed(far_out, sums[half:], top[half:], total[half:])
 
 
-def cross_terms(near, far, samples, prepared):
+def cross_terms(near, far, samples, prepared, picks):
     count, width = samples.shape
     rows = near.shape[0] + far.shape[0]
     part = jax.ShapeDtypeStruct((rows // 2, width + LANES), F32)
     return pl.pallas_call(
-        cross_kernel,
+        functools.partial(cross_kernel, picks),
         out_shape=(part, part),
         in_specs=[VMEM] * (3 + 2 * len(prepared)),
         out_specs=(VMEM, VMEM),
@@ -292,15 +303,15 @@
     )(left, *rights, *more)
 
 
-def self_kernel(near_ref, far_ref, *refs):
+def self_kernel(picks, near_ref, far_ref, *refs):
     visits = (len(refs) - 2) // 2
     visit_refs, centre_ref, out_refs = refs[:visits], refs[visits], refs[visits + 1 :]
     near = near_ref.shape[0]
-    rows = jnp.concatenate([near_ref[...]] + [ref[...] for ref in visit_refs], axis=0)
+    columns = regrouped(near_ref[...], far_ref[...], picks)
+    rows = jnp.concatenate([columns[:near]] + [ref[...] for ref in visit_refs], axis=0)
     wide = rows.astype(F32)
     rows_sq = jnp.sum(wide * wide, axis=1, keepdims=True) * HALF
     scaled = rows * BF16(2.0 * HALF)
-    columns = jnp.concatenate([near_ref[...], far_ref[...]], axis=0)
     dots = lax.dot_general(scaled, columns, NT, preferred_element_type=F32)
     scores = dots - rows_sq - lane_square_norms(columns)[0:1] * HALF
     row_id = lax.broadcasted_iota(jnp.int32, scores.shape, 0)
@@ -317,11 +328,11 @@
         packed(ref, sums[here], top[here], total[here])
 
 
-def self_terms(near, far, visitors, size):
+def self_terms(near, far, visitors, size, picks):
     width = near.shape[1]
     part = jax.ShapeDtypeStruct((size, width + LANES), F32)
     return pl.pallas_call(
-        self_kernel,
+        functools.partial(self_kernel, picks),
         out_shape=(jax.ShapeDtypeStruct(near.shape, F32),) + (part,) * (1 + len(visitors)),
         in_specs=[VMEM] * (2 + len(visitors)),
         out_specs=(VMEM,) * (2 + len(visitors)),
@@ -376,16 +387,16 @@
     assert size == 1 << count and count >= 4
     low, high = 1 << (count - 2), 1 << (count - 1)
     singles = [1] + [(1 << k) | 1 for k in range(1, count - 2)]
-    return singles, [high | low | 1, low, high | 1]
+    return singles, [low | 1, high | low, high | 1], [high | low | 1, low, high | 1]
 
 
 def per_device(particles, samples):
     grp_size = lax.axis_size("grp")
-    singles, triple = swap_masks(lax.axis_size("ref"))
+    singles, gathers, triple = swap_masks(lax.axis_size("ref"))
     count = samples.shape[0]
     own, staged, *first_part = stage(particles, samples, count * STAGED // 4, 8)
     prepared = [first_part]
-    others = [swap(particles, mask) for mask in triple]
+    others = [swap(particles, mask) for mask in gathers]
     block = join([own] + others, 1, first_part[1:])
     prepared += [
         prepare(staged, part * count // 4, count // 4, [block]) for part in range(STAGED, 4)
@@ -393,9 +404,14 @@
     for mask in reversed(singles[1:]):
         block = join([block, swap(block, mask)], 1 + len(triple), prepared[-1][1:])
     far_block = swap(block, singles[0])
-    keep, send = cross_terms(block, far_block, staged, prepared)
+    arrived = [0] + gathers
+    picks = [
+        (0, arrived.index(mask)) if mask in arrived else (1, arrived.index(mask ^ 1))
+        for mask in [0] + triple
+    ]
+    keep, send = cross_terms(block, far_block, staged, prepared, picks)
     visitors = [across(own, k) for k in range(1, grp_size)]
-    centres, *self_parts = self_terms(block, far_block, visitors, own.shape[0])
+    centres, *self_parts = self_terms(block, far_block, visitors, own.shape[0], picks)
     returned = [across(part, -k) for k, part in zip(range(1, grp_size), self_parts[1:])]
     keep, *sends = combine(keep, [swap(send, singles[0])], len(triple), centres)
     rights = [swap(part, mask) for part, mask in zip(sends, triple)]

time: 30.1 us -> 29.9 us (level)
    ppermute x10, starting transfers between devices: 13 us -> 12.7 us  [swap(): return lax.ppermute(values, 'ref', [(i, i ^ mask) for i in range(size)])]
  transfers between devices with their start and end apart: 12 -> 12, of which waited for: 8 -> 7; matrix products, arithmetic and copies ran while one was open for 0% -> 0% of each run, Pallas kernels for 12% -> 12%
where the time goes in v3:
time: 29.9 us; the launch traced here: 29.7 us
  starting transfers between devices  15.7 us (53%)
  waiting for transfers between devices  7.7 us (26%)
  Pallas kernels  6.22 us (21%)
    ppermute x10, starting transfers between devices, swap(): return lax.ppermute(values, 'ref', [(i, i ^ mask) for i in range(size)])  12.7 us
    ppermute x10, waiting for transfers between devices, swap(): return lax.ppermute(values, 'ref', [(i, i ^ mask) for i in range(size)])  5.95 us
    ppermute x2, starting transfers between devices, across(): return lax.ppermute(values, ('grp', 'ref'), pairs)  2.95 us
    pallas_call x1, Pallas kernels, stage(): pl.pallas_call(stage_kernel, out_shape=(pltpu.VMEM(own.shape, own.dtype),...  2.24 us
    pallas_call x1, Pallas kernels, cross_terms(): pl.pallas_call(functools.partial(cross_kernel, picks), out_shape=(part, p...  1.85 us
    ppermute x2, waiting for transfers between devices, across(): return lax.ppermute(values, ('grp', 'ref'), pairs)  1.74 us
    pallas_call x1, Pallas kernels, final(): pl.pallas_call(functools.partial(final_kernel, len(rights)), out_shape=ja...  0.71 us
    pallas_call x2, Pallas kernels, prepare(): pl.pallas_call(functools.partial(prepare_kernel, first), out_shape=(jax.S...  0.69 us
  transfers between devices with their start and end apart: 12, of which 7 were waited for; matrix products, arithmetic and copies ran while one was open for 0% of the time, Pallas kernels for 12%

profile of v3, /device:TPU:0, one launch (start us, length us, event | category | flops | bytes accessed | tf_op | source)
XLA Modules:
  0.0 29.7 jit_solution(7042958697535256639)
XLA Ops:
  0.0 2.5 %collective-permute-start = (bf16[8,512]{1,0:T(8,128)(2,1)}, bf16[8,512]{1,0:T(8,128)(2,1)S(1)}, u32[]{:S(2)}, u32[]{:S(2)}) collective-permute-start(bf16[8,512]{1,0:T(8,128)(2,1)} %own_ref.1), channel_id=1, source_target_pairs={{0,5},{1,4},{2,7},{3,6},{4,1},{5,0},{6,3},{7,2},{8,13},{9,12},{10,... | collective-permute-start | bytes 24584 | tf_op jit(solution)/shard_map/ppermute | solution.py:372
  2.5 2.6 %collective-permute-start.1 = (bf16[8,512]{1,0:T(8,128)(2,1)}, bf16[8,512]{1,0:T(8,128)(2,1)S(1)}, u32[]{:S(2)}, u32[]{:S(2)}) collective-permute-start(bf16[8,512]{1,0:T(8,128)(2,1)} %own_ref.1), channel_id=1, source_target_pairs={{0,12},{1,13},{2,14},{3,15},{4,8},{5,9},{6,10},{7,11},{8,4},{9,5},... | collective-permute-start | bytes 24584 | tf_op jit(solution)/shard_map/ppermute | solution.py:372
  5.1 0.3 collective-permute-start.2
  5.4 2.2 %stage.1 = (bf16[8,512]{1,0:T(8,128)(2,1)S(1)}, bf16[4096,512]{1,0:T(8,128)(2,1)S(1)}, bf16[512,2048]{1,0:T(8,128)(2,1)S(1)}, f32[8,2048]{1,0:T(8,128)S(1)}) custom-call(bf16[8,512]{1,0:T(8,128)(2,1)} %own_ref.1, bf16[4096,512]{1,0:T(8,128)(2,1)} %samples_ref.1), custom_call_target="tpu_custom_call" | custom-call | tf_op jit(solution)/shard_map/stage/pallas_call | solution.py:103
  7.6 0.0 collective-permute-done.refs_1_
  7.6 0.5 %collective-permute-done.1.refs_2_ = bf16[8,512]{1,0:T(8,128)(2,1)S(1)} collective-permute-done((bf16[8,512]{1,0:T(8,128)(2,1)}, bf16[8,512]{1,0:T(8,128)(2,1)S(1)}, u32[]{:S(2)}, u32[]{:S(2)}) %collective-permute-start.1) | collective-permute-done | bytes 8224 | tf_op jit(solution)/shard_map/ppermute | solution.py:372
  8.2 1.1 %collective-permute-done.2.refs_3_ = bf16[8,512]{1,0:T(8,128)(2,1)S(1)} collective-permute-done((bf16[8,512]{1,0:T(8,128)(2,1)}, bf16[8,512]{1,0:T(8,128)(2,1)S(1)}, u32[]{:S(2)}, u32[]{:S(2)}) %collective-permute-start.2) | collective-permute-done | bytes 8224 | tf_op jit(solution)/shard_map/ppermute | solution.py:372
  9.3 1.5 %collective-permute-start.3 = (bf16[32,512]{1,0:T(8,128)(2,1)S(1)}, bf16[32,512]{1,0:T(8,128)(2,1)S(1)}, u32[]{:S(2)}, u32[]{:S(2)}) collective-permute-start(bf16[32,512]{1,0:T(8,128)(2,1)S(1)} %join.2.refs_0_), channel_id=1, source_target_pairs={{0,3},{1,2},{2,1},{3,0},{4,7},{5,6},{6,5},{7,4},{8,11},{9,10},{10,... | collective-permute-start | bytes 98312 | tf_op jit(solution)/shard_map/ppermute | solution.py:372
  10.8 0.3 %prepare.2 = (bf16[512,1024]{1,0:T(8,128)(2,1)S(1)}, f32[8,1024]{1,0:T(8,128)S(1)}) custom-call(bf16[4096,512]{1,0:T(8,128)(2,1)S(1)} %get-tuple-element.26.samples_ref, bf16[32,512]{1,0:T(8,128)(2,1)S(1)} %join.2.refs_0_), custom_call_target="tpu_custom_call" | custom-call | flops 1048576 | bytes 2097152 | tf_op jit(solution)/shard_map/prepare/pallas_call | solution.py:61
  11.1 1.6 %collective-permute-done.3.refs_1_ = bf16[32,512]{1,0:T(8,128)(2,1)S(1)} collective-permute-done((bf16[32,512]{1,0:T(8,128)(2,1)S(1)}, bf16[32,512]{1,0:T(8,128)(2,1)S(1)}, u32[]{:S(2)}, u32[]{:S(2)}) %collective-permute-start.3) | collective-permute-done | bytes 32800 | tf_op jit(solution)/shard_map/ppermute | solution.py:372
  12.7 0.3 %collective-permute-start.4 = (bf16[64,512]{1,0:T(8,128)(2,1)S(1)}, bf16[64,512]{1,0:T(8,128)(2,1)S(1)}, u32[]{:S(2)}, u32[]{:S(2)}) collective-permute-start(bf16[64,512]{1,0:T(8,128)(2,1)S(1)} %join.3.near_ref), channel_id=1, source_target_pairs={{0,1},{1,0},{2,3},{3,2},{4,5},{5,4},{6,7},{7,6},{8,9},{9,8},{10,11... | collective-permute-start | bytes 196616 | tf_op jit(solution)/shard_map/ppermute | solution.py:372
  13.0 0.3 %prepare.3 = (bf16[512,1024]{1,0:T(8,128)(2,1)S(1)}, f32[8,1024]{1,0:T(8,128)S(1)}) custom-call(bf16[4096,512]{1,0:T(8,128)(2,1)S(1)} %get-tuple-element.26.samples_ref, bf16[32,512]{1,0:T(8,128)(2,1)S(1)} %join.2.refs_0_), custom_call_target="tpu_custom_call" | custom-call | flops 1048576 | bytes 2097152 | tf_op jit(solution)/shard_map/prepare/pallas_call | solution.py:61
  13.4 0.6 %collective-permute-done.4.far_ref = bf16[64,512]{1,0:T(8,128)(2,1)S(1)} collective-permute-done((bf16[64,512]{1,0:T(8,128)(2,1)S(1)}, bf16[64,512]{1,0:T(8,128)(2,1)S(1)}, u32[]{:S(2)}, u32[]{:S(2)}) %collective-permute-start.4) | collective-permute-done | bytes 65568 | tf_op jit(solution)/shard_map/ppermute | solution.py:372
  14.0 1.9 %cross_terms.1 = (f32[64,640]{1,0:T(8,128)S(1)}, f32[64,640]{1,0:T(8,128)S(1)}) custom-call(bf16[64,512]{1,0:T(8,128)(2,1)S(1)} %join.3.near_ref, bf16[64,512]{1,0:T(8,128)(2,1)S(1)} %collective-permute-done.4.far_ref, bf16[4096,512]{1,0:T(8,128)(2,1)S(1)} %get-tuple-element.26.samples_ref, bf16[512,2048]{1,0:T(8,128)(2,1)S(1)} %get-tuple-element.28.refs_0_, ...), custom_call_target="tpu_custom_call" | custom-call | flops 1073741824 | bytes 8388608 | tf_op jit(solution)/shard_map/cross_terms/pallas_call | solution.py:198
  15.9 0.3 %collective-permute-start.5 = (f32[64,640]{1,0:T(8,128)S(1)}, f32[64,640]{1,0:T(8,128)S(1)}, u32[]{:S(2)}, u32[]{:S(2)}) collective-permute-start(f32[64,640]{1,0:T(8,128)S(1)} %get-tuple-element.33), channel_id=1, source_target_pairs={{0,1},{1,0},{2,3},{3,2},{4,5},{5,4},{6,7},{7,6},{8,9},{9,8},{10,11... | collective-permute-start | bytes 491528 | tf_op jit(solution)/shard_map/ppermute | solution.py:372
  16.2 1.3 %collective-permute-start.6 = (bf16[8,512]{1,0:T(8,128)(2,1)S(1)}, bf16[8,512]{1,0:T(8,128)(2,1)S(1)}, u32[]{:S(2)}, u32[]{:S(2)}) collective-permute-start(bf16[8,512]{1,0:T(8,128)(2,1)S(1)} %get-tuple-element.24.refs_0_.own_ref), channel_id=1, source_target_pairs={{0,17},{1,16},{2,19},{3,18},{4,21},{5,20},{6,23},{7,22},{8,25},{9,... | collective-permute-start | bytes 24584 | tf_op jit(solution)/shard_map/ppermute | solution.py:382
  17.6 1.7 %collective-permute-done.6.refs_0_ = bf16[8,512]{1,0:T(8,128)(2,1)S(1)} collective-permute-done((bf16[8,512]{1,0:T(8,128)(2,1)S(1)}, bf16[8,512]{1,0:T(8,128)(2,1)S(1)}, u32[]{:S(2)}, u32[]{:S(2)}) %collective-permute-start.6) | collective-permute-done | bytes 8224 | tf_op jit(solution)/shard_map/ppermute | solution.py:382
  19.3 0.5 %self_terms.1 = (f32[64,512]{1,0:T(8,128)S(1)}, f32[8,640]{1,0:T(8,128)S(1)}, f32[8,640]{1,0:T(8,128)S(1)}) custom-call(bf16[64,512]{1,0:T(8,128)(2,1)S(1)} %join.3.near_ref, bf16[64,512]{1,0:T(8,128)(2,1)S(1)} %collective-permute-done.4.far_ref, bf16[8,512]{1,0:T(8,128)(2,1)S(1)} %collective-permute-done.6.refs_0_), custom_call_target="tpu_custom_call" | custom-call | tf_op jit(solution)/shard_map/self_terms/pallas_call | solution.py:334
  19.8 0.0 collective-permute-done.5.right_ref
  19.8 0.1 combine.2
  19.9 1.4 %collective-permute-start.7 = (bf16[16,640]{1,0:T(8,128)(2,1)S(1)}, bf16[16,640]{1,0:T(8,128)(2,1)S(1)}, u32[]{:S(2)}, u32[]{:S(2)}) collective-permute-start(bf16[16,640]{1,0:T(8,128)(2,1)S(1)} %get-tuple-element.36), channel_id=1, source_target_pairs={{0,13},{1,12},{2,15},{3,14},{4,9},{5,8},{6,11},{7,10},{8,5},{9,4},... | collective-permute-start | bytes 61448 | tf_op jit(solution)/shard_map/ppermute | solution.py:372
  21.3 0.0 collective-permute-start.8
  21.3 2.5 %collective-permute-start.9 = (bf16[16,640]{1,0:T(8,128)(2,1)S(1)}, bf16[16,640]{1,0:T(8,128)(2,1)S(1)}, u32[]{:S(2)}, u32[]{:S(2)}) collective-permute-start(bf16[16,640]{1,0:T(8,128)(2,1)S(1)} %get-tuple-element.38), channel_id=1, source_target_pairs={{0,9},{1,8},{2,11},{3,10},{4,13},{5,12},{6,15},{7,14},{8,1},{9,0},... | collective-permute-start | bytes 61448 | tf_op jit(solution)/shard_map/ppermute | solution.py:372
  23.8 1.6 %collective-permute-start.11 = (f32[8,640]{1,0:T(8,128)S(1)}, f32[8,640]{1,0:T(8,128)S(1)}, u32[]{:S(2)}, u32[]{:S(2)}) collective-permute-start(f32[8,640]{1,0:T(8,128)S(1)} %get-tuple-element.42), channel_id=1, source_target_pairs={{0,17},{1,16},{2,19},{3,18},{4,21},{5,20},{6,23},{7,22},{8,25},{9,... | collective-permute-start | bytes 61448 | tf_op jit(solution)/shard_map/ppermute | solution.py:382
  25.4 0.0 collective-permute-done.7.refs_0_
  25.4 0.2 collective-permute-done.8.refs_1_
  25.7 0.0 collective-permute-done.9.refs_2_
  25.7 0.1 combine.3
  25.8 1.3 %collective-permute-start.10 = (bf16[8,640]{1,0:T(8,128)(2,1)S(1)}, bf16[8,640]{1,0:T(8,128)(2,1)S(1)}, u32[]{:S(2)}, u32[]{:S(2)}) collective-permute-start(bf16[8,640]{1,0:T(8,128)(2,1)S(1)} %get-tuple-element.40), channel_id=1, source_target_pairs={{0,3},{1,2},{2,1},{3,0},{4,7},{5,6},{6,5},{7,4},{8,11},{9,10},{10,... | collective-permute-start | bytes 30728 | tf_op jit(solution)/shard_map/ppermute | solution.py:372
  27.1 0.0 collective-permute-done.11.refs_2_
  27.1 1.8 %collective-permute-done.10.refs_0_ = bf16[8,640]{1,0:T(8,128)(2,1)S(1)} collective-permute-done((bf16[8,640]{1,0:T(8,128)(2,1)S(1)}, bf16[8,640]{1,0:T(8,128)(2,1)S(1)}, u32[]{:S(2)}, u32[]{:S(2)}) %collective-permute-start.10) | collective-permute-done | bytes 10272 | tf_op jit(solution)/shard_map/ppermute | solution.py:372
  29.0 0.7 %final.1 = f32[8,512]{1,0:T(8,128)} custom-call(bf16[8,512]{1,0:T(8,128)(2,1)S(1)} %get-tuple-element.24.refs_0_.own_ref, f32[8,640]{1,0:T(8,128)S(1)} %get-tuple-element.39.left_ref, f32[64,512]{1,0:T(8,128)S(1)} %get-tuple-element.34.centre_ref, bf16[8,640]{1,0:T(8,128)(2,1)S(1)} %collective-permute-done.10.refs_0_, ...), custom_call_target="tpu_custom_call" | custom-call | tf_op jit(solution)/shard_map/final/pallas_call | solution.py:360
  (2 shorter events, 0.0 us)
Async XLA Ops:
  0.0 7.6 %collective-permute-start = (bf16[8,512]{1,0:T(8,128)(2,1)}, bf16[8,512]{1,0:T(8,128)(2,1)S(1)}, u32[]{:S(2)}, u32[]{:S(2)}) collective-permute-start(bf16[8,512]{1,0:T(8,128)(2,1)} %own_ref.1), channel_id=1, source_target_pairs={{0,5},{1,4},{2,7},{3,6},{4,1},{5,0},{6,3},{7,2},{8,13},{9,12},{10,... | collective-permute-start | bytes 24584 | tf_op jit(solution)/shard_map/ppermute | solution.py:372
  2.5 5.7 %collective-permute-start.1 = (bf16[8,512]{1,0:T(8,128)(2,1)}, bf16[8,512]{1,0:T(8,128)(2,1)S(1)}, u32[]{:S(2)}, u32[]{:S(2)}) collective-permute-start(bf16[8,512]{1,0:T(8,128)(2,1)} %own_ref.1), channel_id=1, source_target_pairs={{0,12},{1,13},{2,14},{3,15},{4,8},{5,9},{6,10},{7,11},{8,4},{9,5},... | collective-permute-start | bytes 24584 | tf_op jit(solution)/shard_map/ppermute | solution.py:372
  5.1 4.2 %collective-permute-start.2 = (bf16[8,512]{1,0:T(8,128)(2,1)}, bf16[8,512]{1,0:T(8,128)(2,1)S(1)}, u32[]{:S(2)}, u32[]{:S(2)}) collective-permute-start(bf16[8,512]{1,0:T(8,128)(2,1)} %own_ref.1), channel_id=1, source_target_pairs={{0,9},{1,8},{2,11},{3,10},{4,13},{5,12},{6,15},{7,14},{8,1},{9,0},... | collective-permute-start | bytes 24584 | tf_op jit(solution)/shard_map/ppermute | solution.py:372
  9.3 3.4 %collective-permute-start.3 = (bf16[32,512]{1,0:T(8,128)(2,1)S(1)}, bf16[32,512]{1,0:T(8,128)(2,1)S(1)}, u32[]{:S(2)}, u32[]{:S(2)}) collective-permute-start(bf16[32,512]{1,0:T(8,128)(2,1)S(1)} %join.2.refs_0_), channel_id=1, source_target_pairs={{0,3},{1,2},{2,1},{3,0},{4,7},{5,6},{6,5},{7,4},{8,11},{9,10},{10,... | collective-permute-start | bytes 98312 | tf_op jit(solution)/shard_map/ppermute | solution.py:372
  12.7 1.3 %collective-permute-start.4 = (bf16[64,512]{1,0:T(8,128)(2,1)S(1)}, bf16[64,512]{1,0:T(8,128)(2,1)S(1)}, u32[]{:S(2)}, u32[]{:S(2)}) collective-permute-start(bf16[64,512]{1,0:T(8,128)(2,1)S(1)} %join.3.near_ref), channel_id=1, source_target_pairs={{0,1},{1,0},{2,3},{3,2},{4,5},{5,4},{6,7},{7,6},{8,9},{9,8},{10,11... | collective-permute-start | bytes 196616 | tf_op jit(solution)/shard_map/ppermute | solution.py:372
  15.9 3.9 %collective-permute-start.5 = (f32[64,640]{1,0:T(8,128)S(1)}, f32[64,640]{1,0:T(8,128)S(1)}, u32[]{:S(2)}, u32[]{:S(2)}) collective-permute-start(f32[64,640]{1,0:T(8,128)S(1)} %get-tuple-element.33), channel_id=1, source_target_pairs={{0,1},{1,0},{2,3},{3,2},{4,5},{5,4},{6,7},{7,6},{8,9},{9,8},{10,11... | collective-permute-start | bytes 491528 | tf_op jit(solution)/shard_map/ppermute | solution.py:372
  16.2 3.1 %collective-permute-start.6 = (bf16[8,512]{1,0:T(8,128)(2,1)S(1)}, bf16[8,512]{1,0:T(8,128)(2,1)S(1)}, u32[]{:S(2)}, u32[]{:S(2)}) collective-permute-start(bf16[8,512]{1,0:T(8,128)(2,1)S(1)} %get-tuple-element.24.refs_0_.own_ref), channel_id=1, source_target_pairs={{0,17},{1,16},{2,19},{3,18},{4,21},{5,20},{6,23},{7,22},{8,25},{9,... | collective-permute-start | bytes 24584 | tf_op jit(solution)/shard_map/ppermute | solution.py:382
  19.9 5.5 %collective-permute-start.7 = (bf16[16,640]{1,0:T(8,128)(2,1)S(1)}, bf16[16,640]{1,0:T(8,128)(2,1)S(1)}, u32[]{:S(2)}, u32[]{:S(2)}) collective-permute-start(bf16[16,640]{1,0:T(8,128)(2,1)S(1)} %get-tuple-element.36), channel_id=1, source_target_pairs={{0,13},{1,12},{2,15},{3,14},{4,9},{5,8},{6,11},{7,10},{8,5},{9,4},... | collective-permute-start | bytes 61448 | tf_op jit(solution)/shard_map/ppermute | solution.py:372
  21.3 4.4 %collective-permute-start.8 = (bf16[16,640]{1,0:T(8,128)(2,1)S(1)}, bf16[16,640]{1,0:T(8,128)(2,1)S(1)}, u32[]{:S(2)}, u32[]{:S(2)}) collective-permute-start(bf16[16,640]{1,0:T(8,128)(2,1)S(1)} %get-tuple-element.37), channel_id=1, source_target_pairs={{0,4},{1,5},{2,6},{3,7},{4,0},{5,1},{6,2},{7,3},{8,12},{9,13},{10,... | collective-permute-start | bytes 61448 | tf_op jit(solution)/shard_map/ppermute | solution.py:372
  21.3 4.4 %collective-permute-start.9 = (bf16[16,640]{1,0:T(8,128)(2,1)S(1)}, bf16[16,640]{1,0:T(8,128)(2,1)S(1)}, u32[]{:S(2)}, u32[]{:S(2)}) collective-permute-start(bf16[16,640]{1,0:T(8,128)(2,1)S(1)} %get-tuple-element.38), channel_id=1, source_target_pairs={{0,9},{1,8},{2,11},{3,10},{4,13},{5,12},{6,15},{7,14},{8,1},{9,0},... | collective-permute-start | bytes 61448 | tf_op jit(solution)/shard_map/ppermute | solution.py:372
  23.8 3.3 %collective-permute-start.11 = (f32[8,640]{1,0:T(8,128)S(1)}, f32[8,640]{1,0:T(8,128)S(1)}, u32[]{:S(2)}, u32[]{:S(2)}) collective-permute-start(f32[8,640]{1,0:T(8,128)S(1)} %get-tuple-element.42), channel_id=1, source_target_pairs={{0,17},{1,16},{2,19},{3,18},{4,21},{5,20},{6,23},{7,22},{8,25},{9,... | collective-permute-start | bytes 61448 | tf_op jit(solution)/shard_map/ppermute | solution.py:382
  25.8 3.2 %collective-permute-start.10 = (bf16[8,640]{1,0:T(8,128)(2,1)S(1)}, bf16[8,640]{1,0:T(8,128)(2,1)S(1)}, u32[]{:S(2)}, u32[]{:S(2)}) collective-permute-start(bf16[8,640]{1,0:T(8,128)(2,1)S(1)} %get-tuple-element.40), channel_id=1, source_target_pairs={{0,3},{1,2},{2,1},{3,0},{4,7},{5,6},{6,5},{7,4},{8,11},{9,10},{10,... | collective-permute-start | bytes 30728 | tf_op jit(solution)/shard_map/ppermute | solution.py:372

commit v4 on v3

--- a/solution.py
+++ b/solution.py
@@ -16,7 +16,7 @@
 ANY = pl.BlockSpec(memory_space=pl.ANY)
 HBM = pl.BlockSpec(memory_space=pltpu.HBM)
 SMALL = 2 << 20
-STAGED = 2
+STAGED = 3
 F32 = jnp.float32
 BF16 = jnp.bfloat16
 HALF = 1.0 / (2.0 * KERNEL_WIDTH)
@@ -394,15 +394,15 @@
     grp_size = lax.axis_size("grp")
     singles, gathers, triple = swap_masks(lax.axis_size("ref"))
     count = samples.shape[0]
-    own, staged, *first_part = stage(particles, samples, count * STAGED // 4, 8)
+    own, staged, *first_part = stage(particles, samples, count * STAGED // 4, 4)
     prepared = [first_part]
     others = [swap(particles, mask) for mask in gathers]
     block = join([own] + others, 1, first_part[1:])
+    for mask in reversed(singles[1:]):
+        block = join([block, swap(block, mask)], 1 + len(triple))
     prepared += [
         prepare(staged, part * count // 4, count // 4, [block]) for part in range(STAGED, 4)
     ]
-    for mask in reversed(singles[1:]):
-        block = join([block, swap(block, mask)], 1 + len(triple), prepared[-1][1:])
     far_block = swap(block, singles[0])
     arrived = [0] + gathers
     picks = [

time: 29.9 us -> 29.8 us (level)
  Pallas kernels: 6.22 us -> 5.92 us
    pallas_call x2 -> x1, Pallas kernels: 0.69 us -> 0.34 us  [prepare(): pl.pallas_call(functools.partial(prepare_kernel, first), out_shape=(jax.S...]
  transfers between devices with their start and end apart: 12 -> 12, of which waited for: 7 -> 7; matrix products, arithmetic and copies ran while one was open for 0% -> 0% of each run, Pallas kernels for 12% -> 11%
where the time goes in v4:
time: 29.8 us; the launch traced here: 29.6 us
  starting transfers between devices  15.7 us (53%)
  waiting for transfers between devices  7.93 us (27%)
  Pallas kernels  5.92 us (20%)
    ppermute x10, starting transfers between devices, swap(): return lax.ppermute(values, 'ref', [(i, i ^ mask) for i in range(size)])  12.7 us
    ppermute x10, waiting for transfers between devices, swap(): return lax.ppermute(values, 'ref', [(i, i ^ mask) for i in range(size)])  6.19 us
    ppermute x2, starting transfers between devices, across(): return lax.ppermute(values, ('grp', 'ref'), pairs)  2.96 us
    pallas_call x1, Pallas kernels, stage(): pl.pallas_call(stage_kernel, out_shape=(pltpu.VMEM(own.shape, own.dtype),...  2.33 us
    pallas_call x1, Pallas kernels, cross_terms(): pl.pallas_call(functools.partial(cross_kernel, picks), out_shape=(part, p...  1.81 us
    ppermute x2, waiting for transfers between devices, across(): return lax.ppermute(values, ('grp', 'ref'), pairs)  1.74 us
    pallas_call x1, Pallas kernels, final(): pl.pallas_call(functools.partial(final_kernel, len(rights)), out_shape=ja...  0.71 us
  transfers between devices with their start and end apart: 12, of which 7 were waited for; matrix products, arithmetic and copies ran while one was open for 0% of the time, Pallas kernels for 11%

profile of v4, /device:TPU:0, one launch (start us, length us, event | category | flops | bytes accessed | tf_op | source)
XLA Modules:
  0.0 29.6 jit_solution(6328613669278345153)
XLA Ops:
  0.0 2.5 %collective-permute-start = (bf16[8,512]{1,0:T(8,128)(2,1)}, bf16[8,512]{1,0:T(8,128)(2,1)S(1)}, u32[]{:S(2)}, u32[]{:S(2)}) collective-permute-start(bf16[8,512]{1,0:T(8,128)(2,1)} %own_ref.1), channel_id=1, source_target_pairs={{0,5},{1,4},{2,7},{3,6},{4,1},{5,0},{6,3},{7,2},{8,13},{9,12},{10,... | collective-permute-start | bytes 24584 | tf_op jit(solution)/shard_map/ppermute | solution.py:372
  2.5 2.6 %collective-permute-start.1 = (bf16[8,512]{1,0:T(8,128)(2,1)}, bf16[8,512]{1,0:T(8,128)(2,1)S(1)}, u32[]{:S(2)}, u32[]{:S(2)}) collective-permute-start(bf16[8,512]{1,0:T(8,128)(2,1)} %own_ref.1), channel_id=1, source_target_pairs={{0,12},{1,13},{2,14},{3,15},{4,8},{5,9},{6,10},{7,11},{8,4},{9,5},... | collective-permute-start | bytes 24584 | tf_op jit(solution)/shard_map/ppermute | solution.py:372
  5.1 0.3 collective-permute-start.2
  5.4 2.3 %stage.1 = (bf16[8,512]{1,0:T(8,128)(2,1)S(1)}, bf16[4096,512]{1,0:T(8,128)(2,1)S(1)}, bf16[512,3072]{1,0:T(8,128)(2,1)S(1)}, f32[8,3072]{1,0:T(8,128)S(1)}) custom-call(bf16[8,512]{1,0:T(8,128)(2,1)} %own_ref.1, bf16[4096,512]{1,0:T(8,128)(2,1)} %samples_ref.1), custom_call_target="tpu_custom_call" | custom-call | tf_op jit(solution)/shard_map/stage/pallas_call | solution.py:103
  7.7 0.0 collective-permute-done.refs_1_
  7.7 0.4 %collective-permute-done.1.refs_2_ = bf16[8,512]{1,0:T(8,128)(2,1)S(1)} collective-permute-done((bf16[8,512]{1,0:T(8,128)(2,1)}, bf16[8,512]{1,0:T(8,128)(2,1)S(1)}, u32[]{:S(2)}, u32[]{:S(2)}) %collective-permute-start.1) | collective-permute-done | bytes 8224 | tf_op jit(solution)/shard_map/ppermute | solution.py:372
  8.2 1.1 %collective-permute-done.2.refs_3_ = bf16[8,512]{1,0:T(8,128)(2,1)S(1)} collective-permute-done((bf16[8,512]{1,0:T(8,128)(2,1)}, bf16[8,512]{1,0:T(8,128)(2,1)S(1)}, u32[]{:S(2)}, u32[]{:S(2)}) %collective-permute-start.2) | collective-permute-done | bytes 8224 | tf_op jit(solution)/shard_map/ppermute | solution.py:372
  9.3 1.5 %collective-permute-start.3 = (bf16[32,512]{1,0:T(8,128)(2,1)S(1)}, bf16[32,512]{1,0:T(8,128)(2,1)S(1)}, u32[]{:S(2)}, u32[]{:S(2)}) collective-permute-start(bf16[32,512]{1,0:T(8,128)(2,1)S(1)} %join.2.refs_0_), channel_id=1, source_target_pairs={{0,3},{1,2},{2,1},{3,0},{4,7},{5,6},{6,5},{7,4},{8,11},{9,10},{10,... | collective-permute-start | bytes 98312 | tf_op jit(solution)/shard_map/ppermute | solution.py:372
  10.8 1.9 %collective-permute-done.3.refs_1_ = bf16[32,512]{1,0:T(8,128)(2,1)S(1)} collective-permute-done((bf16[32,512]{1,0:T(8,128)(2,1)S(1)}, bf16[32,512]{1,0:T(8,128)(2,1)S(1)}, u32[]{:S(2)}, u32[]{:S(2)}) %collective-permute-start.3) | collective-permute-done | bytes 32800 | tf_op jit(solution)/shard_map/ppermute | solution.py:372
  12.7 0.3 %collective-permute-start.4 = (bf16[64,512]{1,0:T(8,128)(2,1)S(1)}, bf16[64,512]{1,0:T(8,128)(2,1)S(1)}, u32[]{:S(2)}, u32[]{:S(2)}) collective-permute-start(bf16[64,512]{1,0:T(8,128)(2,1)S(1)} %join.3.refs_0_.near_ref), channel_id=1, source_target_pairs={{0,1},{1,0},{2,3},{3,2},{4,5},{5,4},{6,7},{7,6},{8,9},{9,8},{10,11... | collective-permute-start | bytes 196616 | tf_op jit(solution)/shard_map/ppermute | solution.py:372
  13.0 0.3 %prepare.1 = (bf16[512,1024]{1,0:T(8,128)(2,1)S(1)}, f32[8,1024]{1,0:T(8,128)S(1)}) custom-call(bf16[4096,512]{1,0:T(8,128)(2,1)S(1)} %get-tuple-element.24.samples_ref, bf16[64,512]{1,0:T(8,128)(2,1)S(1)} %join.3.refs_0_.near_ref), custom_call_target="tpu_custom_call" | custom-call | flops 1048576 | bytes 2097152 | tf_op jit(solution)/shard_map/prepare/pallas_call | solution.py:61
  13.4 0.6 %collective-permute-done.4.far_ref = bf16[64,512]{1,0:T(8,128)(2,1)S(1)} collective-permute-done((bf16[64,512]{1,0:T(8,128)(2,1)S(1)}, bf16[64,512]{1,0:T(8,128)(2,1)S(1)}, u32[]{:S(2)}, u32[]{:S(2)}) %collective-permute-start.4) | collective-permute-done | bytes 65568 | tf_op jit(solution)/shard_map/ppermute | solution.py:372
  14.0 1.8 %cross_terms.1 = (f32[64,640]{1,0:T(8,128)S(1)}, f32[64,640]{1,0:T(8,128)S(1)}) custom-call(bf16[64,512]{1,0:T(8,128)(2,1)S(1)} %join.3.refs_0_.near_ref, bf16[64,512]{1,0:T(8,128)(2,1)S(1)} %collective-permute-done.4.far_ref, bf16[4096,512]{1,0:T(8,128)(2,1)S(1)} %get-tuple-element.24.samples_ref, bf16[512,3072]{1,0:T(8,128)(2,1)S(1)} %get-tuple-element.25.refs_0_, ...), custom_call_target="tpu_custom_call" | custom-call | flops 1073741824 | bytes 8388608 | tf_op jit(solution)/shard_map/cross_terms/pallas_call | solution.py:198
  15.8 0.3 %collective-permute-start.5 = (f32[64,640]{1,0:T(8,128)S(1)}, f32[64,640]{1,0:T(8,128)S(1)}, u32[]{:S(2)}, u32[]{:S(2)}) collective-permute-start(f32[64,640]{1,0:T(8,128)S(1)} %get-tuple-element.29), channel_id=1, source_target_pairs={{0,1},{1,0},{2,3},{3,2},{4,5},{5,4},{6,7},{7,6},{8,9},{9,8},{10,11... | collective-permute-start | bytes 491528 | tf_op jit(solution)/shard_map/ppermute | solution.py:372
  16.2 1.3 %collective-permute-start.6 = (bf16[8,512]{1,0:T(8,128)(2,1)S(1)}, bf16[8,512]{1,0:T(8,128)(2,1)S(1)}, u32[]{:S(2)}, u32[]{:S(2)}) collective-permute-start(bf16[8,512]{1,0:T(8,128)(2,1)S(1)} %get-tuple-element.22.refs_0_.own_ref), channel_id=1, source_target_pairs={{0,17},{1,16},{2,19},{3,18},{4,21},{5,20},{6,23},{7,22},{8,25},{9,... | collective-permute-start | bytes 24584 | tf_op jit(solution)/shard_map/ppermute | solution.py:382
  17.5 1.7 %collective-permute-done.6.refs_0_ = bf16[8,512]{1,0:T(8,128)(2,1)S(1)} collective-permute-done((bf16[8,512]{1,0:T(8,128)(2,1)S(1)}, bf16[8,512]{1,0:T(8,128)(2,1)S(1)}, u32[]{:S(2)}, u32[]{:S(2)}) %collective-permute-start.6) | collective-permute-done | bytes 8224 | tf_op jit(solution)/shard_map/ppermute | solution.py:382
  19.3 0.5 %self_terms.1 = (f32[64,512]{1,0:T(8,128)S(1)}, f32[8,640]{1,0:T(8,128)S(1)}, f32[8,640]{1,0:T(8,128)S(1)}) custom-call(bf16[64,512]{1,0:T(8,128)(2,1)S(1)} %join.3.refs_0_.near_ref, bf16[64,512]{1,0:T(8,128)(2,1)S(1)} %collective-permute-done.4.far_ref, bf16[8,512]{1,0:T(8,128)(2,1)S(1)} %collective-permute-done.6.refs_0_), custom_call_target="tpu_custom_call" | custom-call | tf_op jit(solution)/shard_map/self_terms/pallas_call | solution.py:334
  19.7 0.0 collective-permute-done.5.right_ref
  19.8 0.1 combine.2
  19.9 1.4 %collective-permute-start.7 = (bf16[16,640]{1,0:T(8,128)(2,1)S(1)}, bf16[16,640]{1,0:T(8,128)(2,1)S(1)}, u32[]{:S(2)}, u32[]{:S(2)}) collective-permute-start(bf16[16,640]{1,0:T(8,128)(2,1)S(1)} %get-tuple-element.32), channel_id=1, source_target_pairs={{0,13},{1,12},{2,15},{3,14},{4,9},{5,8},{6,11},{7,10},{8,5},{9,4},... | collective-permute-start | bytes 61448 | tf_op jit(solution)/shard_map/ppermute | solution.py:372
  21.3 0.1 collective-permute-start.8
  21.4 2.4 %collective-permute-start.9 = (bf16[16,640]{1,0:T(8,128)(2,1)S(1)}, bf16[16,640]{1,0:T(8,128)(2,1)S(1)}, u32[]{:S(2)}, u32[]{:S(2)}) collective-permute-start(bf16[16,640]{1,0:T(8,128)(2,1)S(1)} %get-tuple-element.34), channel_id=1, source_target_pairs={{0,9},{1,8},{2,11},{3,10},{4,13},{5,12},{6,15},{7,14},{8,1},{9,0},... | collective-permute-start | bytes 61448 | tf_op jit(solution)/shard_map/ppermute | solution.py:372
  23.8 1.6 %collective-permute-start.11 = (f32[8,640]{1,0:T(8,128)S(1)}, f32[8,640]{1,0:T(8,128)S(1)}, u32[]{:S(2)}, u32[]{:S(2)}) collective-permute-start(f32[8,640]{1,0:T(8,128)S(1)} %get-tuple-element.38), channel_id=1, source_target_pairs={{0,17},{1,16},{2,19},{3,18},{4,21},{5,20},{6,23},{7,22},{8,25},{9,... | collective-permute-start | bytes 61448 | tf_op jit(solution)/shard_map/ppermute | solution.py:382
  25.4 0.0 collective-permute-done.7.refs_0_
  25.4 0.0 collective-permute-done.8.refs_1_
  25.4 0.2 collective-permute-done.9.refs_2_
  25.6 0.1 combine.3
  25.7 1.3 %collective-permute-start.10 = (bf16[8,640]{1,0:T(8,128)(2,1)S(1)}, bf16[8,640]{1,0:T(8,128)(2,1)S(1)}, u32[]{:S(2)}, u32[]{:S(2)}) collective-permute-start(bf16[8,640]{1,0:T(8,128)(2,1)S(1)} %get-tuple-element.36), channel_id=1, source_target_pairs={{0,3},{1,2},{2,1},{3,0},{4,7},{5,6},{6,5},{7,4},{8,11},{9,10},{10,... | collective-permute-start | bytes 30728 | tf_op jit(solution)/shard_map/ppermute | solution.py:372
  27.1 0.0 collective-permute-done.11.refs_2_
  27.1 1.8 %collective-permute-done.10.refs_0_ = bf16[8,640]{1,0:T(8,128)(2,1)S(1)} collective-permute-done((bf16[8,640]{1,0:T(8,128)(2,1)S(1)}, bf16[8,640]{1,0:T(8,128)(2,1)S(1)}, u32[]{:S(2)}, u32[]{:S(2)}) %collective-permute-start.10) | collective-permute-done | bytes 10272 | tf_op jit(solution)/shard_map/ppermute | solution.py:372
  28.9 0.7 %final.1 = f32[8,512]{1,0:T(8,128)} custom-call(bf16[8,512]{1,0:T(8,128)(2,1)S(1)} %get-tuple-element.22.refs_0_.own_ref, f32[8,640]{1,0:T(8,128)S(1)} %get-tuple-element.35.left_ref, f32[64,512]{1,0:T(8,128)S(1)} %get-tuple-element.30.centre_ref, bf16[8,640]{1,0:T(8,128)(2,1)S(1)} %collective-permute-done.10.refs_0_, ...), custom_call_target="tpu_custom_call" | custom-call | tf_op jit(solution)/shard_map/final/pallas_call | solution.py:360
  (2 shorter events, 0.0 us)
Async XLA Ops:
  0.0 7.7 %collective-permute-start = (bf16[8,512]{1,0:T(8,128)(2,1)}, bf16[8,512]{1,0:T(8,128)(2,1)S(1)}, u32[]{:S(2)}, u32[]{:S(2)}) collective-permute-start(bf16[8,512]{1,0:T(8,128)(2,1)} %own_ref.1), channel_id=1, source_target_pairs={{0,5},{1,4},{2,7},{3,6},{4,1},{5,0},{6,3},{7,2},{8,13},{9,12},{10,... | collective-permute-start | bytes 24584 | tf_op jit(solution)/shard_map/ppermute | solution.py:372
  2.5 5.7 %collective-permute-start.1 = (bf16[8,512]{1,0:T(8,128)(2,1)}, bf16[8,512]{1,0:T(8,128)(2,1)S(1)}, u32[]{:S(2)}, u32[]{:S(2)}) collective-permute-start(bf16[8,512]{1,0:T(8,128)(2,1)} %own_ref.1), channel_id=1, source_target_pairs={{0,12},{1,13},{2,14},{3,15},{4,8},{5,9},{6,10},{7,11},{8,4},{9,5},... | collective-permute-start | bytes 24584 | tf_op jit(solution)/shard_map/ppermute | solution.py:372
  5.1 4.2 %collective-permute-start.2 = (bf16[8,512]{1,0:T(8,128)(2,1)}, bf16[8,512]{1,0:T(8,128)(2,1)S(1)}, u32[]{:S(2)}, u32[]{:S(2)}) collective-permute-start(bf16[8,512]{1,0:T(8,128)(2,1)} %own_ref.1), channel_id=1, source_target_pairs={{0,9},{1,8},{2,11},{3,10},{4,13},{5,12},{6,15},{7,14},{8,1},{9,0},... | collective-permute-start | bytes 24584 | tf_op jit(solution)/shard_map/ppermute | solution.py:372
  9.3 3.4 %collective-permute-start.3 = (bf16[32,512]{1,0:T(8,128)(2,1)S(1)}, bf16[32,512]{1,0:T(8,128)(2,1)S(1)}, u32[]{:S(2)}, u32[]{:S(2)}) collective-permute-start(bf16[32,512]{1,0:T(8,128)(2,1)S(1)} %join.2.refs_0_), channel_id=1, source_target_pairs={{0,3},{1,2},{2,1},{3,0},{4,7},{5,6},{6,5},{7,4},{8,11},{9,10},{10,... | collective-permute-start | bytes 98312 | tf_op jit(solution)/shard_map/ppermute | solution.py:372
  12.7 1.3 %collective-permute-start.4 = (bf16[64,512]{1,0:T(8,128)(2,1)S(1)}, bf16[64,512]{1,0:T(8,128)(2,1)S(1)}, u32[]{:S(2)}, u32[]{:S(2)}) collective-permute-start(bf16[64,512]{1,0:T(8,128)(2,1)S(1)} %join.3.refs_0_.near_ref), channel_id=1, source_target_pairs={{0,1},{1,0},{2,3},{3,2},{4,5},{5,4},{6,7},{7,6},{8,9},{9,8},{10,11... | collective-permute-start | bytes 196616 | tf_op jit(solution)/shard_map/ppermute | solution.py:372
  15.8 3.9 %collective-permute-start.5 = (f32[64,640]{1,0:T(8,128)S(1)}, f32[64,640]{1,0:T(8,128)S(1)}, u32[]{:S(2)}, u32[]{:S(2)}) collective-permute-start(f32[64,640]{1,0:T(8,128)S(1)} %get-tuple-element.29), channel_id=1, source_target_pairs={{0,1},{1,0},{2,3},{3,2},{4,5},{5,4},{6,7},{7,6},{8,9},{9,8},{10,11... | collective-permute-start | bytes 491528 | tf_op jit(solution)/shard_map/ppermute | solution.py:372
  16.2 3.1 %collective-permute-start.6 = (bf16[8,512]{1,0:T(8,128)(2,1)S(1)}, bf16[8,512]{1,0:T(8,128)(2,1)S(1)}, u32[]{:S(2)}, u32[]{:S(2)}) collective-permute-start(bf16[8,512]{1,0:T(8,128)(2,1)S(1)} %get-tuple-element.22.refs_0_.own_ref), channel_id=1, source_target_pairs={{0,17},{1,16},{2,19},{3,18},{4,21},{5,20},{6,23},{7,22},{8,25},{9,... | collective-permute-start | bytes 24584 | tf_op jit(solution)/shard_map/ppermute | solution.py:382
  19.9 5.5 %collective-permute-start.7 = (bf16[16,640]{1,0:T(8,128)(2,1)S(1)}, bf16[16,640]{1,0:T(8,128)(2,1)S(1)}, u32[]{:S(2)}, u32[]{:S(2)}) collective-permute-start(bf16[16,640]{1,0:T(8,128)(2,1)S(1)} %get-tuple-element.32), channel_id=1, source_target_pairs={{0,13},{1,12},{2,15},{3,14},{4,9},{5,8},{6,11},{7,10},{8,5},{9,4},... | collective-permute-start | bytes 61448 | tf_op jit(solution)/shard_map/ppermute | solution.py:372
  21.3 4.1 %collective-permute-start.8 = (bf16[16,640]{1,0:T(8,128)(2,1)S(1)}, bf16[16,640]{1,0:T(8,128)(2,1)S(1)}, u32[]{:S(2)}, u32[]{:S(2)}) collective-permute-start(bf16[16,640]{1,0:T(8,128)(2,1)S(1)} %get-tuple-element.33), channel_id=1, source_target_pairs={{0,4},{1,5},{2,6},{3,7},{4,0},{5,1},{6,2},{7,3},{8,12},{9,13},{10,... | collective-permute-start | bytes 61448 | tf_op jit(solution)/shard_map/ppermute | solution.py:372
  21.4 4.3 %collective-permute-start.9 = (bf16[16,640]{1,0:T(8,128)(2,1)S(1)}, bf16[16,640]{1,0:T(8,128)(2,1)S(1)}, u32[]{:S(2)}, u32[]{:S(2)}) collective-permute-start(bf16[16,640]{1,0:T(8,128)(2,1)S(1)} %get-tuple-element.34), channel_id=1, source_target_pairs={{0,9},{1,8},{2,11},{3,10},{4,13},{5,12},{6,15},{7,14},{8,1},{9,0},... | collective-permute-start | bytes 61448 | tf_op jit(solution)/shard_map/ppermute | solution.py:372
  23.8 3.3 %collective-permute-start.11 = (f32[8,640]{1,0:T(8,128)S(1)}, f32[8,640]{1,0:T(8,128)S(1)}, u32[]{:S(2)}, u32[]{:S(2)}) collective-permute-start(f32[8,640]{1,0:T(8,128)S(1)} %get-tuple-element.38), channel_id=1, source_target_pairs={{0,17},{1,16},{2,19},{3,18},{4,21},{5,20},{6,23},{7,22},{8,25},{9,... | collective-permute-start | bytes 61448 | tf_op jit(solution)/shard_map/ppermute | solution.py:382
  25.7 3.2 %collective-permute-start.10 = (bf16[8,640]{1,0:T(8,128)(2,1)S(1)}, bf16[8,640]{1,0:T(8,128)(2,1)S(1)}, u32[]{:S(2)}, u32[]{:S(2)}) collective-permute-start(bf16[8,640]{1,0:T(8,128)(2,1)S(1)} %get-tuple-element.36), channel_id=1, source_target_pairs={{0,3},{1,2},{2,1},{3,0},{4,7},{5,6},{6,5},{7,4},{8,11},{9,10},{10,... | collective-permute-start | bytes 30728 | tf_op jit(solution)/shard_map/ppermute | solution.py:372
